TPU v7x, 32 devices: a whole 2x2x4 slice. The times are simulated.
32 devices in a mesh: clip: 16 (over z, y, core), frame: 2 (over x).
Axes of the slice: x: 2, y: 2, z: 4, core: 2. Of those that a mesh axis runs over, the one named last changes fastest.
Arguments:
- patch_tokens: bfloat16 [2, 32, 8, 196, 768], P(None, 'clip', 'frame'), may hold values from -6 to 6
- live_slots: int32 [2, 16], P(None, 'clip'), may hold values from 1 to 2, 24 in all within a row
- out_grad: bfloat16 [2, 32, 8, 196, 768], P(None, 'clip', 'frame'), may hold values from -6 to 6
- temporal_gain: bfloat16 [768], P(('clip', 'frame')), may hold values from 0.5 to 1.5
- temporal_shift: bfloat16 [768], P(('clip', 'frame')), may hold values from -1.75 to 1.75
- temporal_in: bfloat16 [768, 2304], P(('clip', 'frame')), may hold values from -0.21875 to 0.21875
- temporal_out: bfloat16 [768, 768], P(('clip', 'frame')), may hold values from -0.4375 to 0.4375
- temporal_bias: bfloat16 [768], P(('clip', 'frame')), may hold values from -1.75 to 1.75
- spatial_gain: bfloat16 [768], P(('clip', 'frame')), may hold values from 0.5 to 1.5
- spatial_shift: bfloat16 [768], P(('clip', 'frame')), may hold values from -1.75 to 1.75
- spatial_in: bfloat16 [768, 2304], P(('clip', 'frame')), may hold values from -0.21875 to 0.21875
- spatial_out: bfloat16 [768, 768], P(('clip', 'frame')), may hold values from -1.25 to 1.25
- spatial_bias: bfloat16 [768], P(('clip', 'frame')), may hold values from -1.75 to 1.75
- mlp_gain: bfloat16 [768], P(('clip', 'frame')), may hold values from 0.5 to 1.5
- mlp_shift: bfloat16 [768], P(('clip', 'frame')), may hold values from -1.75 to 1.75
- expand_weight: bfloat16 [768, 3072], P(('clip', 'frame')), may hold values from -0.21875 to 0.21875
- expand_bias: bfloat16 [3072], P(('clip', 'frame')), may hold values from -3 to 3
- shrink_weight: bfloat16 [3072, 768], P(('clip', 'frame')), may hold values from -0.109375 to 0.109375
- shrink_bias: bfloat16 [768], P(('clip', 'frame')), may hold values from -1.75 to 1.75
Outputs:
- block_out: bfloat16 [2, 32, 8, 196, 768], P(None, 'clip', 'frame')
- patch_grad: bfloat16 [2, 32, 8, 196, 768], P(None, 'clip', 'frame')
- g_temporal_gain: float32 [768], P(('clip', 'frame'))
- g_temporal_shift: float32 [768], P(('clip', 'frame'))
- g_temporal_in: float32 [768, 2304], P(('clip', 'frame'))
- g_temporal_out: float32 [768, 768], P(('clip', 'frame'))
- g_temporal_bias: float32 [768], P(('clip', 'frame'))
- g_spatial_gain: float32 [768], P(('clip', 'frame'))
- g_spatial_shift: float32 [768], P(('clip', 'frame'))
- g_spatial_in: float32 [768, 2304], P(('clip', 'frame'))
- g_spatial_out: float32 [768, 768], P(('clip', 'frame'))
- g_spatial_bias: float32 [768], P(('clip', 'frame'))
- g_mlp_gain: float32 [768], P(('clip', 'frame'))
- g_mlp_shift: float32 [768], P(('clip', 'frame'))
- g_expand_weight: float32 [768, 3072], P(('clip', 'frame'))
- g_expand_bias: float32 [3072], P(('clip', 'frame'))
- g_shrink_weight: float32 [3072, 768], P(('clip', 'frame'))
- g_shrink_bias: float32 [768], P(('clip', 'frame'))
Inputs may be any that keep to these rules, and one draw needn't show every extreme that they name: `live_slots`: slot c of a group of clip holds a clip in micro-batch m if c is below the entry; each micro-batch holds 24 clips, and in each some group holds 2.
All inputs are finite; a program needn't handle non-finite values.
Results may differ from a plain program's by a relative error of at most 0.019.
Values may be sent and summed in bfloat16 or wider, within the bound.
A program may use at most 280 MiB of HBM per device.

v0:
```python
import jax
import jax.numpy as jnp
from jax import lax
from jax.sharding import PartitionSpec as P

H = 12
DH = 64


def layer_norm(values, gain, shift):
    centre = values - jnp.mean(values, -1, keepdims=True)
    spread = jnp.mean(centre * centre, -1, keepdims=True)
    return centre * lax.rsqrt(spread + 1e-06) * gain + shift


def exact_gelu(values):
    return jax.nn.gelu(values, approximate=False)


def rows_product(left, right):
    return lax.dot_general(
        left, right, (((0,), (0,)), ((), ())), preferred_element_type=jnp.float32
    )


def back_product(grads_in, weight):
    return lax.dot_general(
        grads_in, weight, (((1,), (1,)), ((), ())), preferred_element_type=jnp.float32
    )


def forward_dot(left, right):
    return jnp.dot(left, right, preferred_element_type=jnp.float32)


def softmax_parts(scores):
    top_value = jnp.max(scores, -1, keepdims=True)
    expo_value = jnp.exp(scores - top_value)
    total_value = jnp.sum(expo_value, -1, keepdims=True)
    return (expo_value / total_value, top_value + jnp.log(total_value))


def softmax_back(probs, grad_probs):
    return (probs * (grad_probs - jnp.sum(probs * grad_probs, -1, keepdims=True))).astype(
        jnp.bfloat16
    )


def to_patch_rows(values, slot_count, local_frames, patch_count):
    width = values.shape[-1]
    return (
        values.reshape(slot_count, local_frames, patch_count, width)
        .transpose(0, 2, 1, 3)
        .reshape(slot_count * patch_count, local_frames, width)
    )


def from_patch_rows(values, slot_count, local_frames, patch_count):
    width = values.shape[-1]
    return (
        values.reshape(slot_count, patch_count, local_frames, width)
        .transpose(0, 2, 1, 3)
        .reshape(slot_count * local_frames * patch_count, width)
    )


def micro_batch(weights, tokens, out_cot, count):
    (
        temporal_gain,
        temporal_shift,
        temporal_in,
        temporal_out,
        temporal_bias,
        spatial_gain,
        spatial_shift,
        spatial_in,
        spatial_out,
        spatial_bias,
        mlp_gain,
        mlp_shift,
        expand_weight,
        expand_bias,
        shrink_weight,
        shrink_bias,
    ) = weights
    slot_count, local_frames, patch_count, model_width = tokens.shape
    row_count = slot_count * local_frames * patch_count
    head_shape = (slot_count, local_frames, patch_count, H, DH)
    live_mask = (jnp.arange(slot_count) < count).astype(jnp.float32)[:, None, None, None]
    cotan = (out_cot.astype(jnp.float32) * live_mask).reshape(row_count, model_width)
    flat_in = tokens.astype(jnp.float32).reshape(row_count, model_width)
    normed_t, norm_t_back = jax.vjp(
        layer_norm, flat_in, temporal_gain.astype(jnp.float32), temporal_shift.astype(jnp.float32)
    )
    normed_t = normed_t.astype(jnp.bfloat16)
    packed_t = forward_dot(normed_t, temporal_in).astype(jnp.bfloat16)
    frame_rows = lax.all_to_all(
        to_patch_rows(packed_t, slot_count, local_frames, patch_count),
        "frame",
        split_axis=0,
        concat_axis=1,
        tiled=True,
    )
    row_part, all_frames = (frame_rows.shape[0], frame_rows.shape[1])
    split_shape = (row_part, all_frames, H, DH)
    query_x = frame_rows[:, :, :model_width].reshape(split_shape)
    key_x = frame_rows[:, :, model_width : 2 * model_width].reshape(split_shape)
    value_x = frame_rows[:, :, 2 * model_width :].reshape(split_shape)
    scores_x = (
        jnp.einsum("rfhd,rghd->rhfg", query_x, key_x, preferred_element_type=jnp.float32) * 0.125
    )
    probs_x, lse_x = softmax_parts(scores_x)
    mixed_x = jnp.einsum(
        "rhfg,rghd->rfhd", probs_x.astype(jnp.bfloat16), value_x, preferred_element_type=jnp.float32
    )
    mixed_x = mixed_x.astype(jnp.bfloat16).reshape(row_part, all_frames, model_width)
    mixed_back = lax.all_to_all(mixed_x, "frame", split_axis=1, concat_axis=0, tiled=True)
    mixed_t = from_patch_rows(mixed_back, slot_count, local_frames, patch_count)
    after_time = flat_in + forward_dot(mixed_t, temporal_out) + temporal_bias.astype(jnp.float32)
    normed_s, norm_s_back = jax.vjp(
        layer_norm, after_time, spatial_gain.astype(jnp.float32), spatial_shift.astype(jnp.float32)
    )
    normed_s = normed_s.astype(jnp.bfloat16)
    packed_s = (
        forward_dot(normed_s, spatial_in)
        .astype(jnp.bfloat16)
        .reshape(slot_count, local_frames, patch_count, 3, H, DH)
    )
    query_s = packed_s[:, :, :, 0]
    key_s = packed_s[:, :, :, 1]
    value_s = packed_s[:, :, :, 2]
    scores_s = (
        jnp.einsum("cfphd,cfrhd->cfhpr", query_s, key_s, preferred_element_type=jnp.float32) * 0.125
    )
    probs_s, lse_s = softmax_parts(scores_s)
    mixed_s = jnp.einsum(
        "cfhpr,cfrhd->cfphd",
        probs_s.astype(jnp.bfloat16),
        value_s,
        preferred_element_type=jnp.float32,
    )
    mixed_s = mixed_s.astype(jnp.bfloat16).reshape(row_count, model_width)
    after_space = after_time + forward_dot(mixed_s, spatial_out) + spatial_bias.astype(jnp.float32)
    normed_m, norm_m_back = jax.vjp(
        layer_norm, after_space, mlp_gain.astype(jnp.float32), mlp_shift.astype(jnp.float32)
    )
    normed_m = normed_m.astype(jnp.bfloat16)
    hidden = forward_dot(normed_m, expand_weight) + expand_bias.astype(jnp.float32)
    active, gelu_back = jax.vjp(exact_gelu, hidden)
    active = active.astype(jnp.bfloat16)
    block_rows = after_space + forward_dot(active, shrink_weight) + shrink_bias.astype(jnp.float32)
    grad_z = cotan.astype(jnp.bfloat16)
    g_shrink_weight = rows_product(active, grad_z)
    g_shrink_bias = jnp.sum(grad_z.astype(jnp.float32), 0)
    grad_hidden = gelu_back(back_product(grad_z, shrink_weight))[0].astype(jnp.bfloat16)
    g_expand_weight = rows_product(normed_m, grad_hidden)
    g_expand_bias = jnp.sum(grad_hidden.astype(jnp.float32), 0)
    space_grad, g_mlp_gain, g_mlp_shift = norm_m_back(back_product(grad_hidden, expand_weight))
    space_grad = cotan + space_grad
    grad_ys = space_grad.astype(jnp.bfloat16)
    g_spatial_out = rows_product(mixed_s, grad_ys)
    g_spatial_bias = jnp.sum(grad_ys.astype(jnp.float32), 0)
    grad_mixed_s = back_product(grad_ys, spatial_out).astype(jnp.bfloat16).reshape(head_shape)
    again_s = jnp.exp(
        jnp.einsum("cfphd,cfrhd->cfhpr", query_s, key_s, preferred_element_type=jnp.float32) * 0.125
        - lse_s
    )
    grad_probs_s = jnp.einsum(
        "cfphd,cfrhd->cfhpr", grad_mixed_s, value_s, preferred_element_type=jnp.float32
    )
    grad_scores_s = softmax_back(again_s, grad_probs_s)
    grad_query_s = (
        jnp.einsum("cfhpr,cfrhd->cfphd", grad_scores_s, key_s, preferred_element_type=jnp.float32)
        * 0.125
    ).astype(jnp.bfloat16)
    grad_key_s = (
        jnp.einsum("cfhpr,cfphd->cfrhd", grad_scores_s, query_s, preferred_element_type=jnp.float32)
        * 0.125
    ).astype(jnp.bfloat16)
    grad_value_s = jnp.einsum(
        "cfhpr,cfphd->cfrhd",
        again_s.astype(jnp.bfloat16),
        grad_mixed_s,
        preferred_element_type=jnp.float32,
    ).astype(jnp.bfloat16)
    grad_packed_s = jnp.stack([grad_query_s, grad_key_s, grad_value_s], axis=3).reshape(
        row_count, 3 * model_width
    )
    g_spatial_in = rows_product(normed_s, grad_packed_s)
    time_grad, g_spatial_gain, g_spatial_shift = norm_s_back(
        back_product(grad_packed_s, spatial_in)
    )
    time_grad = space_grad + time_grad
    grad_yt = time_grad.astype(jnp.bfloat16)
    g_temporal_out = rows_product(mixed_t, grad_yt)
    g_temporal_bias = jnp.sum(grad_yt.astype(jnp.float32), 0)
    grad_mixed_flat = back_product(grad_yt, temporal_out).astype(jnp.bfloat16)
    grad_rows = lax.all_to_all(
        to_patch_rows(grad_mixed_flat, slot_count, local_frames, patch_count),
        "frame",
        split_axis=0,
        concat_axis=1,
        tiled=True,
    )
    grad_mixed_x = grad_rows.reshape(split_shape)
    again_x = jnp.exp(
        jnp.einsum("rfhd,rghd->rhfg", query_x, key_x, preferred_element_type=jnp.float32) * 0.125
        - lse_x
    )
    grad_probs_x = jnp.einsum(
        "rfhd,rghd->rhfg", grad_mixed_x, value_x, preferred_element_type=jnp.float32
    )
    grad_scores_x = softmax_back(again_x, grad_probs_x)
    grad_query_x = (
        jnp.einsum("rhfg,rghd->rfhd", grad_scores_x, key_x, preferred_element_type=jnp.float32)
        * 0.125
    ).astype(jnp.bfloat16)
    grad_key_x = (
        jnp.einsum("rhfg,rfhd->rghd", grad_scores_x, query_x, preferred_element_type=jnp.float32)
        * 0.125
    ).astype(jnp.bfloat16)
    grad_value_x = jnp.einsum(
        "rhfg,rfhd->rghd",
        again_x.astype(jnp.bfloat16),
        grad_mixed_x,
        preferred_element_type=jnp.float32,
    ).astype(jnp.bfloat16)
    packed_width = (row_part, all_frames, model_width)
    grad_stacked = jnp.concatenate(
        [
            grad_query_x.reshape(packed_width),
            grad_key_x.reshape(packed_width),
            grad_value_x.reshape(packed_width),
        ],
        axis=2,
    )
    grad_back = lax.all_to_all(grad_stacked, "frame", split_axis=1, concat_axis=0, tiled=True)
    grad_packed_t = from_patch_rows(grad_back, slot_count, local_frames, patch_count)
    g_temporal_in = rows_product(normed_t, grad_packed_t)
    input_grad, g_temporal_gain, g_temporal_shift = norm_t_back(
        back_product(grad_packed_t, temporal_in)
    )
    input_grad = time_grad + input_grad
    grads = (
        g_temporal_gain,
        g_temporal_shift,
        g_temporal_in,
        g_temporal_out,
        g_temporal_bias,
        g_spatial_gain,
        g_spatial_shift,
        g_spatial_in,
        g_spatial_out,
        g_spatial_bias,
        g_mlp_gain,
        g_mlp_shift,
        g_expand_weight,
        g_expand_bias,
        g_shrink_weight,
        g_shrink_bias,
    )
    return (
        block_rows.astype(jnp.bfloat16).reshape(tokens.shape),
        input_grad.astype(jnp.bfloat16).reshape(tokens.shape),
        grads,
    )


def body(
    patch_tokens,
    live_slots,
    out_grad,
    temporal_gain,
    temporal_shift,
    temporal_in,
    temporal_out,
    temporal_bias,
    spatial_gain,
    spatial_shift,
    spatial_in,
    spatial_out,
    spatial_bias,
    mlp_gain,
    mlp_shift,
    expand_weight,
    expand_bias,
    shrink_weight,
    shrink_bias,
):
    shards = (
        temporal_gain,
        temporal_shift,
        temporal_in,
        temporal_out,
        temporal_bias,
        spatial_gain,
        spatial_shift,
        spatial_in,
        spatial_out,
        spatial_bias,
        mlp_gain,
        mlp_shift,
        expand_weight,
        expand_bias,
        shrink_weight,
        shrink_bias,
    )
    devices = lax.axis_size("clip") * lax.axis_size("frame")
    start = tuple(
        (
            jnp.zeros((member.shape[0] * devices,) + member.shape[1:], jnp.float32)
            for member in shards
        )
    )

    def one_step(totals, inputs):
        tokens, out_cot, count = inputs
        weights = (
            lax.all_gather(temporal_gain, ("clip", "frame"), axis=0, tiled=True),
            lax.all_gather(temporal_shift, ("clip", "frame"), axis=0, tiled=True),
            lax.all_gather(temporal_in, ("clip", "frame"), axis=0, tiled=True),
            lax.all_gather(temporal_out, ("clip", "frame"), axis=0, tiled=True),
            lax.all_gather(temporal_bias, ("clip", "frame"), axis=0, tiled=True),
            lax.all_gather(spatial_gain, ("clip", "frame"), axis=0, tiled=True),
            lax.all_gather(spatial_shift, ("clip", "frame"), axis=0, tiled=True),
            lax.all_gather(spatial_in, ("clip", "frame"), axis=0, tiled=True),
            lax.all_gather(spatial_out, ("clip", "frame"), axis=0, tiled=True),
            lax.all_gather(spatial_bias, ("clip", "frame"), axis=0, tiled=True),
            lax.all_gather(mlp_gain, ("clip", "frame"), axis=0, tiled=True),
            lax.all_gather(mlp_shift, ("clip", "frame"), axis=0, tiled=True),
            lax.all_gather(expand_weight, ("clip", "frame"), axis=0, tiled=True),
            lax.all_gather(expand_bias, ("clip", "frame"), axis=0, tiled=True),
            lax.all_gather(shrink_weight, ("clip", "frame"), axis=0, tiled=True),
            lax.all_gather(shrink_bias, ("clip", "frame"), axis=0, tiled=True),
        )
        block_part, grad_part, grads = micro_batch(weights, tokens, out_cot, count)
        totals = tuple((summed + addend for summed, addend in zip(totals, grads)))
        return (totals, (block_part, grad_part))

    totals, outputs = lax.scan(one_step, start, (patch_tokens, out_grad, live_slots[:, 0]))
    block_out, patch_grad = outputs
    totals = (
        lax.psum_scatter(totals[0], ("clip", "frame"), scatter_dimension=0, tiled=True),
        lax.psum_scatter(totals[1], ("clip", "frame"), scatter_dimension=0, tiled=True),
        lax.psum_scatter(totals[2], ("clip", "frame"), scatter_dimension=0, tiled=True),
        lax.psum_scatter(totals[3], ("clip", "frame"), scatter_dimension=0, tiled=True),
        lax.psum_scatter(totals[4], ("clip", "frame"), scatter_dimension=0, tiled=True),
        lax.psum_scatter(totals[5], ("clip", "frame"), scatter_dimension=0, tiled=True),
        lax.psum_scatter(totals[6], ("clip", "frame"), scatter_dimension=0, tiled=True),
        lax.psum_scatter(totals[7], ("clip", "frame"), scatter_dimension=0, tiled=True),
        lax.psum_scatter(totals[8], ("clip", "frame"), scatter_dimension=0, tiled=True),
        lax.psum_scatter(totals[9], ("clip", "frame"), scatter_dimension=0, tiled=True),
        lax.psum_scatter(totals[10], ("clip", "frame"), scatter_dimension=0, tiled=True),
        lax.psum_scatter(totals[11], ("clip", "frame"), scatter_dimension=0, tiled=True),
        lax.psum_scatter(totals[12], ("clip", "frame"), scatter_dimension=0, tiled=True),
        lax.psum_scatter(totals[13], ("clip", "frame"), scatter_dimension=0, tiled=True),
        lax.psum_scatter(totals[14], ("clip", "frame"), scatter_dimension=0, tiled=True),
        lax.psum_scatter(totals[15], ("clip", "frame"), scatter_dimension=0, tiled=True),
    )
    return (block_out, patch_grad) + tuple(totals)


def solution(mesh):
    placed = (
        P(None, "clip", "frame", None, None),
        P(None, "clip"),
        P(None, "clip", "frame", None, None),
        P(("clip", "frame")),
        P(("clip", "frame")),
        P(("clip", "frame"), None),
        P(("clip", "frame"), None),
        P(("clip", "frame")),
        P(("clip", "frame")),
        P(("clip", "frame")),
        P(("clip", "frame"), None),
        P(("clip", "frame"), None),
        P(("clip", "frame")),
        P(("clip", "frame")),
        P(("clip", "frame")),
        P(("clip", "frame"), None),
        P(("clip", "frame")),
        P(("clip", "frame"), None),
        P(("clip", "frame")),
    )
    return jax.shard_map(
        body,
        mesh=mesh,
        in_specs=placed,
        out_specs=(
            P(None, "clip", "frame", None, None),
            P(None, "clip", "frame", None, None),
            P(("clip", "frame")),
            P(("clip", "frame")),
            P(("clip", "frame"), None),
            P(("clip", "frame"), None),
            P(("clip", "frame")),
            P(("clip", "frame")),
            P(("clip", "frame")),
            P(("clip", "frame"), None),
            P(("clip", "frame"), None),
            P(("clip", "frame")),
            P(("clip", "frame")),
            P(("clip", "frame")),
            P(("clip", "frame"), None),
            P(("clip", "frame")),
            P(("clip", "frame"), None),
            P(("clip", "frame")),
        ),
        check_vma=False,
    )
```

profile of v0, /device:TPU:0, one launch (start us, length us, event | category | flops | bytes accessed | tf_op | source)
XLA Modules:
  0.0 2755.7 jit_solution(523773952191247082)
XLA Ops:
  8.2 1998.5 %while.45 = (s32[]{:T(128)}, f32[768]{0:T(1024)}, f32[768]{0:T(1024)}, f32[768,2304]{1,0:T(8,128)}, f32[768,768]{1,0:T(8,128)}, /*index=5*/f32[768]{0:T(1024)}, ...) while((s32[]{:T(128)}, f32[768]{0:T(1024)}, ...), condition=%wide.region_29.30_spmd.clone, body=%wide.region_0.29_spmd.clone.sunk | while | flops 92436963328 | bytes 1525417088 | solution.py:340
  20.2 42.8 %all-reduce.33 = (bf16[768]{0:T(1024)(128)(2,1)S(1)}, bf16[768]{0:T(1024)(128)(2,1)S(1)}, bf16[768]{0:T(1024)(128)(2,1)S(1)}, bf16[768]{0:T(1024)(128)(2,1)S(1)}...) all-reduce(bf16[768]{0:T(1024)(128)(2,1)S(1)} %dynamic-update-slice, ...), channel_id=1, replica_groups=mesh['clip'=16,'frame'=2] {'clip','frame'}, use_global_device_ids=true, to_apply=%add.1 | all-reduce | flops 9984 | bytes 39936 | tf_op jit(solution)/shard_map/while
  122.6 79.1 %all-to-all-done = bf16[392,4,2304]{2,1,0:T(4,128)(2,1)} async-done(((bf16[392,4,2304]{2,1,0:T(4,128)(2,1)}), bf16[392,4,2304]{2,1,0:T(4,128)(2,1)}, u32[]{:S(2)}, u32[]{:S(2)}) %all-to-all-start) | async-done | bytes 7225376 | tf_op jit(solution)/shard_map/while/body/eval_jaxpr/all_to_all | solution.py:97
  307.2 24.6 all-to-all-done.1
  354.8 22.5 reshape.341
  468.0 54.7 %multiply_convert_fusion.16 = (bf16[1568,3072]{1,0:T(8,128)(2,1)}, f32[1568,3072]{1,0:T(8,128)}, f32[1568,3072]{1,0:T(8,128)}) fusion(f32[3072]{0:T(1024)S(1)} %copy-done.43, bf16[768,3072]{1,0:T(8,128)(2,1)} %all-gather.15.cloned.1.call-done, f32[1568,768]{1,0:T(8,128)} %copy-done.2, f32[768]{0:T(1024)S(1)} %copy-done.27, f32[768]{0:T(1024)S(1)} %copy-done.18, ...), kind=kOutput, calls=%fused_computation.7.clone.2 | convolution fusion | flops 7722688512 | bytes 57735424 | tf_op jit(solution)/shard_map/while/body/eval_jaxpr/dot_general | solution.py:33
  522.7 25.5 convert_reduce_fusion.11
  683.7 16.7 reshape.345
  906.8 55.0 %all-to-all-done.3 = bf16[196,8,2304]{2,0,1:T(8,128)(2,1)} async-done(((bf16[196,8,2304]{2,0,1:T(8,128)(2,1)}), bf16[196,8,2304]{2,0,1:T(8,128)(2,1)}, u32[]{:S(2)}, u32[]{:S(2)}) %all-to-all-start.3) | async-done | bytes 7225376 | tf_op jit(solution)/shard_map/while/body/eval_jaxpr/all_to_all | solution.py:237
  1019.9 38.0 %all-reduce.33 = (bf16[768]{0:T(1024)(128)(2,1)S(1)}, bf16[768]{0:T(1024)(128)(2,1)S(1)}, bf16[768]{0:T(1024)(128)(2,1)S(1)}, bf16[768]{0:T(1024)(128)(2,1)S(1)}...) all-reduce(bf16[768]{0:T(1024)(128)(2,1)S(1)} %dynamic-update-slice, ...), channel_id=1, replica_groups=mesh['clip'=16,'frame'=2] {'clip','frame'}, use_global_device_ids=true, to_apply=%add.1 | all-reduce | flops 9984 | bytes 39936 | tf_op jit(solution)/shard_map/while
  1117.0 79.1 %all-to-all-done = bf16[392,4,2304]{2,1,0:T(4,128)(2,1)} async-done(((bf16[392,4,2304]{2,1,0:T(4,128)(2,1)}), bf16[392,4,2304]{2,1,0:T(4,128)(2,1)}, u32[]{:S(2)}, u32[]{:S(2)}) %all-to-all-start) | async-done | bytes 7225376 | tf_op jit(solution)/shard_map/while/body/eval_jaxpr/all_to_all | solution.py:97
  1301.5 24.3 all-to-all-done.1
  1348.8 22.5 reshape.341
  1462.0 54.7 %multiply_convert_fusion.16 = (bf16[1568,3072]{1,0:T(8,128)(2,1)}, f32[1568,3072]{1,0:T(8,128)}, f32[1568,3072]{1,0:T(8,128)}) fusion(f32[3072]{0:T(1024)S(1)} %copy-done.43, bf16[768,3072]{1,0:T(8,128)(2,1)} %all-gather.15.cloned.1.call-done, f32[1568,768]{1,0:T(8,128)} %copy-done.2, f32[768]{0:T(1024)S(1)} %copy-done.27, f32[768]{0:T(1024)S(1)} %copy-done.18, ...), kind=kOutput, calls=%fused_computation.7.clone.2 | convolution fusion | flops 7722688512 | bytes 57735424 | tf_op jit(solution)/shard_map/while/body/eval_jaxpr/dot_general | solution.py:33
  1516.8 25.5 convert_reduce_fusion.11
  1887.3 17.0 select_add_fusion.38
  1904.3 53.1 %all-to-all-done.3 = bf16[196,8,2304]{2,0,1:T(8,128)(2,1)} async-done(((bf16[196,8,2304]{2,0,1:T(8,128)(2,1)}), bf16[196,8,2304]{2,0,1:T(8,128)(2,1)}, u32[]{:S(2)}, u32[]{:S(2)}) %all-to-all-start.3) | async-done | bytes 7225376 | tf_op jit(solution)/shard_map/while/body/eval_jaxpr/all_to_all | solution.py:237
  2010.9 41.1 %all-reduce.31 = (f32[768]{0:T(1024)S(1)}, f32[768]{0:T(1024)S(1)}, f32[768]{0:T(1024)S(1)}, f32[768]{0:T(1024)S(1)}, f32[768]{0:T(1024)S(1)}, /*index=5*/f32[76...) all-reduce(f32[768]{0:T(1024)S(1)} %copy-done.70, ...), channel_id=2, replica_groups=mesh['clip'=16,'frame'=2] {'clip','frame'}, use_global_device_ids=true, to_apply=%region_30.31.clone | all-reduce | flops 9984 | bytes 79872
  2057.8 53.1 %reduce-scatter.9.cloned.1.call-done = f32[24,768]{1,0:T(8,128)} async-done(((f32[768,768]{1,0:T(8,128)}), f32[24,768]{1,0:T(8,128)}) %reduce-scatter.9.cloned.1.call-update) | async-done | bytes 73744 | tf_op jit(solution)/shard_map/reduce_scatter | solution.py:346
  2110.9 104.4 %reduce-scatter.13.cloned.1.call-done = f32[24,768]{1,0:T(8,128)} async-done(((f32[768,768]{1,0:T(8,128)}), f32[24,768]{1,0:T(8,128)}) %reduce-scatter.13.cloned.1.call-update) | async-done | bytes 73744 | tf_op jit(solution)/shard_map/reduce_scatter | solution.py:351
  2215.3 124.6 %reduce-scatter.7.cloned.1.call-done = f32[24,2304]{1,0:T(8,128)} async-done(((f32[768,2304]{1,0:T(8,128)}), f32[24,2304]{1,0:T(8,128)}) %reduce-scatter.7.cloned.1.call-update) | async-done | bytes 221200 | tf_op jit(solution)/shard_map/reduce_scatter | solution.py:345
  2339.8 124.8 %reduce-scatter.11.cloned.1.call-done = f32[24,2304]{1,0:T(8,128)} async-done(((f32[768,2304]{1,0:T(8,128)}), f32[24,2304]{1,0:T(8,128)}) %reduce-scatter.11.cloned.1.call-update) | async-done | bytes 221200 | tf_op jit(solution)/shard_map/reduce_scatter | solution.py:350
  2464.6 141.7 %reduce-scatter.15.cloned.1.call-done = f32[24,3072]{1,0:T(8,128)} async-done(((f32[768,3072]{1,0:T(8,128)}), f32[24,3072]{1,0:T(8,128)}) %reduce-scatter.15.cloned.1.call-update) | async-done | bytes 294928 | tf_op jit(solution)/shard_map/reduce_scatter | solution.py:355
  2606.3 141.7 %reduce-scatter.17.cloned.1.call-done = f32[96,768]{1,0:T(8,128)} async-done(((f32[3072,768]{1,0:T(8,128)}), f32[96,768]{1,0:T(8,128)}) %reduce-scatter.17.cloned.1.call-update) | async-done | bytes 294928 | tf_op jit(solution)/shard_map/reduce_scatter | solution.py:357
  (726 shorter events, 1368.0 us)
Async XLA Ops:
  8.4 66.9 %all-gather.7.cloned.1.call-start = ((), (), s32[]{:S(2)}) async-start(), calls=%async_computation.16 | async-start | bytes 3649536 | tf_op jit(solution)/shard_map/while/body/eval_jaxpr/all_gather | solution.py:321
  9.2 325.3 %all-gather.9.cloned.1.call-start = ((), (), s32[]{:S(2)}) async-start(), calls=%async_computation.17 | async-start | bytes 1216512 | tf_op jit(solution)/shard_map/while/body/eval_jaxpr/all_gather | solution.py:322
  9.9 333.8 %all-gather.11.cloned.1.call-start = ((), (), s32[]{:S(2)}) async-start(), calls=%async_computation.18 | async-start | bytes 3649536 | tf_op jit(solution)/shard_map/while/body/eval_jaxpr/all_gather | solution.py:326
  10.7 448.0 %all-gather.13.cloned.1.call-start = ((), (), s32[]{:S(2)}) async-start(), calls=%async_computation.19 | async-start | bytes 1216512 | tf_op jit(solution)/shard_map/while/body/eval_jaxpr/all_gather | solution.py:327
  11.2 456.7 %all-gather.15.cloned.1.call-start = ((), (), s32[]{:S(2)}) async-start(), calls=%async_computation.20 | async-start | bytes 4866048 | tf_op jit(solution)/shard_map/while/body/eval_jaxpr/all_gather | solution.py:331
  102.1 99.6 %all-to-all-start = ((bf16[392,4,2304]{2,1,0:T(4,128)(2,1)}), bf16[392,4,2304]{2,1,0:T(4,128)(2,1)}, u32[]{:S(2)}, u32[]{:S(2)}) async-start(bf16[392,4,2304]{2,1,0:T(4,128)(2,1)} %bitcast.280), calls=%async_computation | async-start | bytes 14450688 | tf_op jit(solution)/shard_map/while/body/eval_jaxpr/all_to_all | solution.py:97
  108.8 413.9 %all-gather.17.cloned.1.call-start = ((), (), s32[]{:S(2)}) async-start(), calls=%async_computation.21 | async-start | bytes 4866048 | tf_op jit(solution)/shard_map/while/body/eval_jaxpr/all_gather | solution.py:333
  290.0 41.9 %all-to-all-start.1 = ((bf16[196,8,768]{2,0,1:T(8,128)(2,1)}), bf16[196,8,768]{2,0,1:T(8,128)(2,1)}, u32[]{:S(2)}, u32[]{:S(2)}) async-start(bf16[196,8,768]{2,0,1:T(8,128)(2,1)} %copy.260), calls=%async_computation.1 | async-start | bytes 4915200 | tf_op jit(solution)/shard_map/while/body/eval_jaxpr/all_to_all | solution.py:117
  874.7 87.2 %all-to-all-start.3 = ((bf16[196,8,2304]{2,0,1:T(8,128)(2,1)}), bf16[196,8,2304]{2,0,1:T(8,128)(2,1)}, u32[]{:S(2)}, u32[]{:S(2)}) async-start(bf16[196,8,2304]{2,0,1:T(8,128)(2,1)} %copy.273), calls=%async_computation.3 | async-start | bytes 14745600 | tf_op jit(solution)/shard_map/while/body/eval_jaxpr/all_to_all | solution.py:237
  1008.0 61.8 %all-gather.7.cloned.1.call-start = ((), (), s32[]{:S(2)}) async-start(), calls=%async_computation.16 | async-start | bytes 3649536 | tf_op jit(solution)/shard_map/while/body/eval_jaxpr/all_gather | solution.py:321
  1008.7 319.8 %all-gather.9.cloned.1.call-start = ((), (), s32[]{:S(2)}) async-start(), calls=%async_computation.17 | async-start | bytes 1216512 | tf_op jit(solution)/shard_map/while/body/eval_jaxpr/all_gather | solution.py:322
  1009.5 328.3 %all-gather.11.cloned.1.call-start = ((), (), s32[]{:S(2)}) async-start(), calls=%async_computation.18 | async-start | bytes 3649536 | tf_op jit(solution)/shard_map/while/body/eval_jaxpr/all_gather | solution.py:326
  1010.2 442.5 %all-gather.13.cloned.1.call-start = ((), (), s32[]{:S(2)}) async-start(), calls=%async_computation.19 | async-start | bytes 1216512 | tf_op jit(solution)/shard_map/while/body/eval_jaxpr/all_gather | solution.py:327
  1010.8 451.2 %all-gather.15.cloned.1.call-start = ((), (), s32[]{:S(2)}) async-start(), calls=%async_computation.20 | async-start | bytes 4866048 | tf_op jit(solution)/shard_map/while/body/eval_jaxpr/all_gather | solution.py:331
  1096.6 99.5 %all-to-all-start = ((bf16[392,4,2304]{2,1,0:T(4,128)(2,1)}), bf16[392,4,2304]{2,1,0:T(4,128)(2,1)}, u32[]{:S(2)}, u32[]{:S(2)}) async-start(bf16[392,4,2304]{2,1,0:T(4,128)(2,1)} %bitcast.280), calls=%async_computation | async-start | bytes 14450688 | tf_op jit(solution)/shard_map/while/body/eval_jaxpr/all_to_all | solution.py:97
  1103.3 413.4 %all-gather.17.cloned.1.call-start = ((), (), s32[]{:S(2)}) async-start(), calls=%async_computation.21 | async-start | bytes 4866048 | tf_op jit(solution)/shard_map/while/body/eval_jaxpr/all_gather | solution.py:333
  1284.3 41.5 %all-to-all-start.1 = ((bf16[196,8,768]{2,0,1:T(8,128)(2,1)}), bf16[196,8,768]{2,0,1:T(8,128)(2,1)}, u32[]{:S(2)}, u32[]{:S(2)}) async-start(bf16[196,8,768]{2,0,1:T(8,128)(2,1)} %copy.260), calls=%async_computation.1 | async-start | bytes 4915200 | tf_op jit(solution)/shard_map/while/body/eval_jaxpr/all_to_all | solution.py:117
  1870.4 86.9 %all-to-all-start.3 = ((bf16[196,8,2304]{2,0,1:T(8,128)(2,1)}), bf16[196,8,2304]{2,0,1:T(8,128)(2,1)}, u32[]{:S(2)}, u32[]{:S(2)}) async-start(bf16[196,8,2304]{2,0,1:T(8,128)(2,1)} %copy.273), calls=%async_computation.3 | async-start | bytes 14745600 | tf_op jit(solution)/shard_map/while/body/eval_jaxpr/all_to_all | solution.py:237
  2006.7 104.2 %reduce-scatter.9.cloned.1.call-start = ((), (), s32[]{:S(2)}) async-start(), calls=%async_computation.11 | async-start | bytes 2433024 | tf_op jit(solution)/shard_map/reduce_scatter | solution.py:346
  2007.3 208.0 %reduce-scatter.13.cloned.1.call-start = ((), (), s32[]{:S(2)}) async-start(), calls=%async_computation.13 | async-start | bytes 2433024 | tf_op jit(solution)/shard_map/reduce_scatter | solution.py:351
  2007.9 332.0 %reduce-scatter.7.cloned.1.call-start = ((), (), s32[]{:S(2)}) async-start(), calls=%async_computation.10 | async-start | bytes 7299072 | tf_op jit(solution)/shard_map/reduce_scatter | solution.py:345
  2008.4 456.2 %reduce-scatter.11.cloned.1.call-start = ((), (), s32[]{:S(2)}) async-start(), calls=%async_computation.12 | async-start | bytes 7299072 | tf_op jit(solution)/shard_map/reduce_scatter | solution.py:350
  2009.2 597.2 %reduce-scatter.15.cloned.1.call-start = ((), (), s32[]{:S(2)}) async-start(), calls=%async_computation.14 | async-start | bytes 9732096 | tf_op jit(solution)/shard_map/reduce_scatter | solution.py:355
  2010.0 738.0 %reduce-scatter.17.cloned.1.call-start = ((), (), s32[]{:S(2)}) async-start(), calls=%async_computation.15 | async-start | bytes 9732096 | tf_op jit(solution)/shard_map/reduce_scatter | solution.py:357
  (171 other events, 2861.6 us)
Sparse Core Ops, SparseCore 0:
  12.2 63.0 all-gather.6
  78.2 54.1 all-gather.8
  135.4 66.8 all-gather.10
  205.0 52.8 all-gather.12
  260.7 70.6 all-gather.14
  334.1 62.4 all-gather.16
  1011.7 57.6 all-gather.6
  1072.4 54.2 all-gather.8
  1129.5 66.7 all-gather.10
  1199.1 52.8 all-gather.12
  1254.9 70.6 all-gather.14
  1328.3 62.3 all-gather.16
Sparse Core Ops, SparseCore 1:
  2013.0 97.8 reduce-scatter.8
  2116.6 98.6 reduce-scatter.12
  2221.4 118.4 reduce-scatter.6
  2346.1 118.5 reduce-scatter.10
  2471.1 135.2 reduce-scatter.14
  2612.8 135.2 reduce-scatter.16
where the time goes:
time: 2770 us; the launch traced here: 2760 us
  waiting for transfers between devices  1020 us (37%)
  matrix products  738 us (27%)
  local copies, waits for them, and re-layouts  611 us (22%)
  other arithmetic  190 us (7%)
  blocking collectives  122 us (4%)
  starting transfers between devices  49 us (2%)
    dot_general x12, matrix products, forward_dot(): return jnp.dot(left, right, preferred_element_type=jnp.float32)  203 us
    all_to_all x2, waiting for transfers between devices, micro_batch(): lax.all_to_all(to_patch_rows(packed_t, slot_count, local_frames, patch_co...  158 us
    dot_general x12, matrix products, back_product(): lax.dot_general(grads_in, weight, (((1,), (1,)), ((), ())), preferred_ele...  148 us
    dot_general x12, matrix products, rows_product(): lax.dot_general(left, right, (((0,), (0,)), ((), ())), preferred_element_...  146 us
    reduce_scatter x1, waiting for transfers between devices, body(): lax.psum_scatter(totals[14], ('clip', 'frame'), scatter_dimension=0, tile...  142 us
    reduce_scatter x1, waiting for transfers between devices, body(): lax.psum_scatter(totals[12], ('clip', 'frame'), scatter_dimension=0, tile...  142 us
    reduce_scatter x1, waiting for transfers between devices, body(): lax.psum_scatter(totals[7], ('clip', 'frame'), scatter_dimension=0, tiled...  125 us
    reduce_scatter x1, waiting for transfers between devices, body(): lax.psum_scatter(totals[2], ('clip', 'frame'), scatter_dimension=0, tiled...  125 us
  transfers between devices with their start and end apart: 26, of which 15 were waited for; matrix products, arithmetic and copies ran while one was open for 29% of the time, Pallas kernels for 0%

commit v1 on v0

--- a/solution.py
+++ b/solution.py
@@ -1,10 +1,26 @@
 import jax
 import jax.numpy as jnp
 from jax import lax
+from jax.experimental import pallas as pl
+from jax.experimental.pallas import tpu as pltpu
 from jax.sharding import PartitionSpec as P
 
 H = 12
 DH = 64
+D = 768
+PATCHES = 196
+ROWS = 208
+PAIR = 2
+HALF = 4
+TILE = PAIR * ROWS
+GROUP = 3
+CHUNK = 768
+CHUNKS = 4
+BLOCK = 16
+BLOCKS = ROWS // BLOCK
+VMEM_BYTES = 66 * 1000 * 1000
+bf16 = jnp.bfloat16
+f32 = jnp.float32
 
 
 def layer_norm(values, gain, shift):
@@ -266,7 +282,7 @@
     )
 
 
-def body(
+def generic_body(
     patch_tokens,
     live_slots,
     out_grad,
@@ -360,6 +376,875 @@
     return (block_out, patch_grad) + tuple(totals)
 
 
+def nn(left, right):
+    return lax.dot_general(left, right, (((1,), (0,)), ((), ())), preferred_element_type=f32)
+
+
+def nt(left, right):
+    return lax.dot_general(left, right, (((1,), (1,)), ((), ())), preferred_element_type=f32)
+
+
+def tn(left, right):
+    return lax.dot_general(left, right, (((0,), (0,)), ((), ())), preferred_element_type=f32)
+
+
+TAIL_POLE = 0.275
+TAIL = (0.11782574, 0.04201021, 0.33417963, -0.33129375, 0.45218007, -0.1149019)
+
+
+def gelu_parts(u):
+    bell = jnp.exp(u * u * -0.5)
+    t = 1.0 / (1.0 + TAIL_POLE * jnp.abs(u))
+    poly = jnp.full_like(t, TAIL[5])
+    for term in TAIL[4::-1]:
+        poly = poly * t + term
+    tail = poly * t * bell
+    cdf = jnp.where(u >= 0, 1.0 - tail, tail)
+    return u * cdf, cdf + u * (bell * 0.3989422804014327)
+
+
+def norm_parts(v):
+    centre = v - jnp.mean(v, -1, keepdims=True)
+    r = lax.rsqrt(jnp.mean(centre * centre, -1, keepdims=True) + 1e-06)
+    return centre * r, r
+
+
+def norm_back(a, n, r, gain):
+    scaled = a * gain
+    return r * (
+        scaled
+        - jnp.mean(scaled, -1, keepdims=True)
+        - n * jnp.mean(scaled * n, -1, keepdims=True)
+    )
+
+
+def column_sum(values):
+    return jnp.sum(values, 0, keepdims=True)
+
+
+def halves(pair):
+    lane = lax.broadcasted_iota(jnp.int32, pair.shape, 1)
+    zero = jnp.zeros_like(pair)
+    return jnp.where(lane < DH, pair, zero), jnp.where(lane < DH, zero, pair)
+
+
+def stacked(pair):
+    return jnp.concatenate(halves(pair), axis=0)
+
+
+T_GAIN, T_SHIFT, T_BIAS, S_GAIN, S_SHIFT, S_BIAS, M_GAIN, M_SHIFT, M_BIAS, HIDDEN = range(10)
+
+
+def row_of(ref, at):
+    return ref[at : at + 1, :]
+
+
+def lanes(start, size):
+    return pl.ds(pl.multiple_of(start, size), size)
+
+
+def temporal_forward_kernel(
+    slot_ref, own_ref, other_ref, vec_ref, win_ref,
+    packed_ref, probs_ref, mixed_own_ref, mixed_other_ref, pad_s,
+):
+    pad_s[...] = jnp.zeros_like(pad_s)
+    gain, shift = row_of(vec_ref, T_GAIN), row_of(vec_ref, T_SHIFT)
+    for half, tokens_ref in enumerate((own_ref, other_ref)):
+
+        def project(i, carry, half=half, tokens_ref=tokens_ref):
+            for f in range(PAIR):
+                pad_s[f, :PATCHES] = tokens_ref[PAIR * i + f]
+            n, _ = norm_parts(pad_s[...].reshape(TILE, D).astype(f32))
+            normed = (n * gain + shift).astype(bf16)
+            at = pl.ds(half * 4 + PAIR * i, PAIR)
+            packed_ref[at] = nn(normed, win_ref[...]).astype(bf16).reshape(PAIR, ROWS, 3 * D)
+            return carry
+
+        lax.fori_loop(0, 4 // PAIR, project, 0)
+
+    row = lax.broadcasted_iota(jnp.int32, (8 * BLOCK, 8 * BLOCK), 0) % BLOCK
+    col = lax.broadcasted_iota(jnp.int32, (8 * BLOCK, 8 * BLOCK), 1) % BLOCK
+    same = row == col
+
+    def attend(b, carry):
+        at = pl.ds(pl.multiple_of(b * BLOCK, BLOCK), BLOCK)
+        def part(h, k):
+            lo = k * D + 128 * h
+            return packed_ref[:, at, lo : lo + 128].reshape(8 * BLOCK, 128)
+
+        scores, both = [], []
+        for h in range(H // 2):
+            query = part(h, 0) * jnp.asarray(0.125, bf16)
+            scores.append(nt(query, stacked(part(h, 1))))
+        for h in range(H // 2):
+            probs = []
+            for k in range(2):
+                s = jnp.where(same, scores[h][:, 128 * k : 128 * k + 128], -1e30)
+                e = jnp.exp(s - jnp.max(s, -1, keepdims=True))
+                probs.append(e * (1.0 / jnp.sum(e, -1, keepdims=True)))
+            both.append(jnp.concatenate(probs, axis=1).astype(bf16))
+            probs_ref[b, h] = both[h]
+        for h in range(H // 2):
+            mixed = nn(both[h], stacked(part(h, 2))).astype(bf16).reshape(8, BLOCK, 128)
+            mixed_own_ref[:, at, 128 * h : 128 * h + 128] = mixed[:4]
+            mixed_other_ref[:, at, 128 * h : 128 * h + 128] = mixed[4:]
+        return carry
+
+    lax.fori_loop(0, BLOCKS, attend, 0)
+
+
+def fixed(shape, at=None):
+    at = at or (0,) * len(shape)
+    return pl.BlockSpec(shape, lambda *ids: at, pipeline_mode=pl.Buffered(1))
+
+
+def out_of(shape, kind):
+    return jax.ShapeDtypeStruct(shape, kind)
+
+
+def temporal_forward(slot, tokens, other, vec, weights):
+    mbs = tokens.shape[0]
+    frames = tokens.shape[2]
+    own = pl.BlockSpec((None, None, frames, PATCHES, D), lambda m, s: (m, s[0], 0, 0, 0))
+    mixed = pl.BlockSpec((None, frames, ROWS, D), lambda m, s: (m, 0, 0, 0))
+    return pl.pallas_call(
+        temporal_forward_kernel,
+        grid_spec=pltpu.PrefetchScalarGridSpec(
+            num_scalar_prefetch=1,
+            grid=(mbs,),
+            in_specs=[
+                own,
+                pl.BlockSpec((None, frames, PATCHES, D), lambda m, s: (m, 0, 0, 0)),
+                fixed((16, D)),
+                fixed((D, 3 * D)),
+            ],
+            out_specs=[
+                pl.BlockSpec((None, 8, ROWS, 3 * D), lambda m, s: (m, 0, 0, 0)),
+                pl.BlockSpec((None, BLOCKS, H // 2, 128, 256), lambda m, s: (m, 0, 0, 0, 0)),
+                mixed,
+                mixed,
+            ],
+            scratch_shapes=[pltpu.VMEM((PAIR, ROWS, D), bf16)],
+        ),
+        out_shape=[
+            out_of((mbs, 8, ROWS, 3 * D), bf16),
+            out_of((mbs, BLOCKS, H // 2, 128, 256), bf16),
+            out_of((mbs, frames, ROWS, D), bf16),
+            out_of((mbs, frames, ROWS, D), bf16),
+        ],
+        compiler_params=pltpu.CompilerParams(vmem_limit_bytes=VMEM_BYTES),
+        cost_estimate=pl.CostEstimate(
+            flops=2 * mbs * 8 * ROWS * D * 4 * D, bytes_accessed=60 << 20, transcendentals=0
+        ),
+        name="temporal_forward",
+    )(slot, tokens, other, vec, weights)
+
+
+def spatial_forward_kernel(*refs):
+    slot_ref, tokens_ref, mixed_ref, vec_ref, tout_ref, sin_ref, sout_ref = refs[:7]
+    time_ref, packed_ref, probs_ref, mixs_ref, space_ref, pad_s = refs[-6:]
+    pad_s[...] = jnp.zeros_like(pad_s)
+    for f in range(PAIR):
+        pad_s[f, :PATCHES] = tokens_ref[f]
+    tokens = pad_s[...].reshape(TILE, D).astype(f32)
+    time = tokens + nn(mixed_ref[...].reshape(TILE, D), tout_ref[...]) + row_of(vec_ref, T_BIAS)
+    time_ref[...] = time.reshape(PAIR, ROWS, D)
+    n, _ = norm_parts(time)
+    normed = (n * row_of(vec_ref, S_GAIN) + row_of(vec_ref, S_SHIFT)).astype(bf16)
+    packed_ref[...] = nn(normed, sin_ref[...]).astype(bf16).reshape(PAIR, ROWS, 3 * D)
+    valid = lax.broadcasted_iota(jnp.int32, (ROWS, ROWS), 1) < PATCHES
+
+    def attend(g, carry):
+        both = [(f, GROUP * g + i) for i in range(GROUP) for f in range(PAIR)]
+
+        def part(f, h, k):
+            return packed_ref[f, :, lanes(k * D + 128 * h, 128)]
+
+        scores, probs = [], []
+        for f, h in both:
+            query = part(f, h, 0) * jnp.asarray(0.125, bf16)
+            scores += [nt(query, keys) for keys in halves(part(f, h, 1))]
+        for i, s in enumerate(scores):
+            f, h = both[i // 2]
+            s = jnp.where(valid, s, -1e30)
+            e = jnp.exp(s - jnp.max(s, -1, keepdims=True))
+            probs.append((e * (1.0 / jnp.sum(e, -1, keepdims=True))).astype(bf16))
+            probs_ref[f, 2 * h + i % 2] = probs[i]
+        for i, (f, h) in enumerate(both):
+            low, high = halves(part(f, h, 2))
+            total = nn(probs[2 * i], low) + nn(probs[2 * i + 1], high)
+            mixs_ref[f, :, lanes(128 * h, 128)] = total.astype(bf16)
+        return carry
+
+    lax.fori_loop(0, H // 2 // GROUP, attend, 0)
+    mixed = mixs_ref[...].reshape(TILE, D)
+    space_ref[...] = (
+        time_ref[...].reshape(TILE, D) + nn(mixed, sout_ref[...]) + row_of(vec_ref, S_BIAS)
+    ).reshape(PAIR, ROWS, D)
+
+
+def spatial_forward(which, slot, tokens, mixed, vec, second, earlier):
+    mbs, slots, frames = tokens.shape[:3]
+
+    def framed(*tail):
+        return pl.BlockSpec(
+            (None, None, PAIR) + tail, lambda m, i, s: (which, m, i) + (0,) * len(tail)
+        )
+
+    def whole(*tail):
+        return (slots, mbs, frames) + tail
+
+    shapes = [
+        out_of(whole(ROWS, D), f32),
+        out_of(whole(ROWS, 3 * D), bf16),
+        out_of(whole(H, ROWS, ROWS), bf16),
+        out_of(whole(ROWS, D), bf16),
+        out_of(whole(ROWS, D), f32),
+    ]
+    return pl.pallas_call(
+        spatial_forward_kernel,
+        grid_spec=pltpu.PrefetchScalarGridSpec(
+            num_scalar_prefetch=1,
+            grid=(mbs, frames // PAIR),
+            in_specs=[
+                pl.BlockSpec(
+                    (None, None, PAIR, PATCHES, D), lambda m, i, s: (m, s[which], i, 0, 0)
+                ),
+                pl.BlockSpec((None, PAIR, ROWS, D), lambda m, i, s: (m, i, 0, 0)),
+                fixed((16, D)),
+                fixed((D, D), (0, 3)),
+                fixed((D, 3 * D)),
+                fixed((D, D), (0, 4)),
+            ]
+            + [pl.BlockSpec(memory_space=pl.ANY)] * len(earlier),
+            out_specs=[
+                framed(ROWS, D),
+                framed(ROWS, 3 * D),
+                framed(H, ROWS, ROWS),
+                framed(ROWS, D),
+                framed(ROWS, D),
+            ],
+            scratch_shapes=[pltpu.VMEM((PAIR, ROWS, D), bf16)],
+        ),
+        out_shape=shapes,
+        input_output_aliases={7 + i: i for i in range(len(earlier))},
+        compiler_params=pltpu.CompilerParams(vmem_limit_bytes=VMEM_BYTES),
+        cost_estimate=pl.CostEstimate(
+            flops=2 * mbs * frames * ROWS * D * 6 * D, bytes_accessed=60 << 20, transcendentals=0
+        ),
+        name="spatial_forward",
+    )(slot, tokens, mixed, vec, second, second, second, *earlier)
+
+
+def mlp_kernel(
+    slot_ref, live_ref, space_ref, cotan_ref, vec_ref, hidden_ref, expand_ref, shrink_ref,
+    out_ref, grad_ref, weights_ref, sums_ref, hidden_sums_ref,
+    z_s, normed_s, total_s, back_s, expand_s, shrink_s,
+):
+    i = pl.program_id(0)
+
+    @pl.when(i == 0)
+    def _():
+        expand_s[...] = jnp.zeros_like(expand_s)
+        shrink_s[...] = jnp.zeros_like(shrink_s)
+        sums_ref[...] = jnp.zeros_like(sums_ref)
+        hidden_sums_ref[...] = jnp.zeros_like(hidden_sums_ref)
+        z_s[...] = jnp.zeros_like(z_s)
+
+    gain = row_of(vec_ref, M_GAIN)
+    live = live_ref[i]
+    for f in range(PAIR):
+        cotan = cotan_ref[f]
+        z_s[f, :PATCHES] = jnp.where(live > 0, cotan, jnp.zeros_like(cotan))
+    grad_z = z_s[...].reshape(TILE, D)
+    space = space_ref[...].reshape(TILE, D)
+    n, _ = norm_parts(space)
+    normed = (n * gain + row_of(vec_ref, M_SHIFT)).astype(bf16)
+    normed_s[...] = normed
+    total_s[...] = space + row_of(vec_ref, M_BIAS)
+    back_s[...] = jnp.zeros_like(back_s)
+    normed_turned = normed.T
+    z_turned = grad_z.T
+
+    def ahead(j):
+        at = slice(j * CHUNK, (j + 1) * CHUNK)
+        hidden = nn(normed_s[...], expand_ref[:, at]) + hidden_ref[:, at]
+        return hidden, nt(grad_z, shrink_ref[:, at])
+
+    pending = ahead(0)
+    for j in range(CHUNKS):
+        at = slice(j * CHUNK, (j + 1) * CHUNK)
+        hidden, grad_active = pending
+        if j + 1 < CHUNKS:
+            pending = ahead(j + 1)
+        active, slope = gelu_parts(hidden)
+        active = active.astype(bf16)
+        grad_hidden = (slope * grad_active).astype(bf16)
+        total_s[...] += nn(active, shrink_ref[:, at])
+        shrink_s[:, at] += nn(z_turned, active)
+        expand_s[:, at] += nn(normed_turned, grad_hidden)
+        back_s[...] += nt(grad_hidden, expand_ref[:, at])
+        hidden_sums_ref[0:1, at] += column_sum(grad_hidden.astype(f32))
+    block_out = total_s[...].reshape(PAIR, ROWS, D)
+    for f in range(PAIR):
+        out_ref[f] = block_out[f, :PATCHES].astype(bf16)
+    a = back_s[...]
+    n, r = norm_parts(space_ref[...].reshape(TILE, D))
+    wide_z = grad_z.astype(f32)
+    grad_ref[...] = (wide_z + norm_back(a, n, r, gain)).reshape(PAIR, ROWS, D)
+    sums_ref[0:1] += column_sum(a * n)
+    sums_ref[1:2] += column_sum(a)
+    sums_ref[2:3] += column_sum(wide_z)
+
+    @pl.when(i == pl.num_programs(0) - 1)
+    def _():
+        weights_ref[:, : CHUNKS * CHUNK] = expand_s[...].astype(bf16)
+        for j in range(CHUNKS):
+            lo = j * CHUNK
+            weights_ref[:, CHUNKS * CHUNK + lo : CHUNKS * CHUNK + lo + D] = (
+                shrink_s[:, lo : lo + CHUNK].T.astype(bf16)
+            )
+
+
+def mlp(slot, live, space, cotan, vec, hidden, third):
+    slots, mbs, frames = space.shape[:3]
+    per = frames // PAIR
+    steps = slots * mbs * per
+
+    def placed(i):
+        return i // (mbs * per), (i // per) % mbs, i % per
+
+    def by_slot(i, s, live):
+        r, m, f = placed(i)
+        return m, s[r], f, 0, 0
+
+    def framed(i, s, live):
+        return placed(i) + (0, 0)
+
+    outer = pl.BlockSpec((None, None, PAIR, PATCHES, D), by_slot)
+    inner = pl.BlockSpec((None, None, PAIR, ROWS, D), framed)
+    width = CHUNKS * CHUNK
+    return pl.pallas_call(
+        mlp_kernel,
+        grid_spec=pltpu.PrefetchScalarGridSpec(
+            num_scalar_prefetch=2,
+            grid=(steps,),
+            in_specs=[
+                inner,
+                outer,
+                fixed((16, D)),
+                fixed((1, width)),
+                fixed((D, width), (0, 0)),
+                fixed((D, width), (0, 1)),
+            ],
+            out_specs=[
+                outer,
+                inner,
+                fixed((D, 2 * width)),
+                fixed((8, D)),
+                fixed((8, width)),
+            ],
+            scratch_shapes=[
+                pltpu.VMEM((PAIR, ROWS, D), bf16),
+                pltpu.VMEM((TILE, D), bf16),
+                pltpu.VMEM((TILE, D), f32),
+                pltpu.VMEM((TILE, D), f32),
+                pltpu.VMEM((D, width), f32),
+                pltpu.VMEM((D, width), f32),
+            ],
+        ),
+        out_shape=[
+            out_of(cotan.shape, bf16),
+            out_of(space.shape, f32),
+            out_of((D, 2 * width), bf16),
+            out_of((8, D), f32),
+            out_of((8, width), f32),
+        ],
+        compiler_params=pltpu.CompilerParams(vmem_limit_bytes=VMEM_BYTES),
+        cost_estimate=pl.CostEstimate(
+            flops=12 * steps * TILE * D * width, bytes_accessed=60 << 20, transcendentals=0
+        ),
+        name="mlp",
+    )(slot, live, space, cotan, vec, hidden, third, third)
+
+
+def spatial_backward_kernel(first_call, *refs):
+    (
+        grad_ref, packed_ref, probs_ref, mixs_ref, time_ref, mixed_ref,
+        vec_ref, tout_ref, sin_ref, sout_ref,
+    ) = refs[:10]
+    if first_call:
+        weights_ref, sums_ref, time_grad_ref, back_ref, gmix_s, gpack_s = refs[-6:]
+        in_acc = out_acc = tail_acc = None
+        total = weights_ref
+    else:
+        total_ref, sums_before_ref = refs[10:12]
+        weights_ref, sums_ref, time_grad_ref, back_ref, gmix_s, gpack_s, total = refs[-7:]
+    step = pl.program_id(0) * pl.num_programs(1) + pl.program_id(1)
+    steps = pl.num_programs(0) * pl.num_programs(1)
+
+    @pl.when(step == 0)
+    def _():
+        if first_call:
+            total[...] = jnp.zeros_like(total)
+            sums_ref[...] = jnp.zeros_like(sums_ref)
+        else:
+            pltpu.sync_copy(total_ref, total)
+            sums_ref[...] = sums_before_ref[...]
+
+    gain = row_of(vec_ref, S_GAIN)
+    space_grad = grad_ref[...].reshape(TILE, D)
+    grad_ys = space_grad.astype(bf16)
+    total[:, 3 * D : 4 * D] += tn(mixs_ref[...].reshape(TILE, D), grad_ys)
+    gmix_s[...] = nt(grad_ys, sout_ref[...]).astype(bf16).reshape(PAIR, ROWS, D)
+
+    def attend(g, carry):
+        both = [(f, GROUP * g + i) for i in range(GROUP) for f in range(PAIR)]
+
+        def part(f, h, k):
+            return packed_ref[f, :, lanes(k * D + 128 * h, 128)]
+
+        products, scores = [], []
+        for f, h in both:
+            out_pair = gmix_s[f, :, lanes(128 * h, 128)]
+            products += [nt(out_pair, values) for values in halves(part(f, h, 2))]
+        for i, product in enumerate(products):
+            f, h = both[i // 2]
+            wide = probs_ref[f, 2 * h + i % 2].astype(f32)
+            product = wide * product
+            scores.append(
+                (product - wide * jnp.sum(product, -1, keepdims=True)).astype(bf16)
+            )
+        for i, (f, h) in enumerate(both):
+            outs = halves(gmix_s[f, :, lanes(128 * h, 128)])
+            queries, keys = halves(part(f, h, 0)), halves(part(f, h, 1))
+            near = scores[2 * i : 2 * i + 2]
+            grad_v = tn(probs_ref[f, 2 * h], outs[0]) + tn(probs_ref[f, 2 * h + 1], outs[1])
+            grad_q = nn(near[0], keys[0]) + nn(near[1], keys[1])
+            grad_k = tn(near[0], queries[0]) + tn(near[1], queries[1])
+            gpack_s[f, :, lanes(128 * h, 128)] = (grad_q * 0.125).astype(bf16)
+            gpack_s[f, :, lanes(D + 128 * h, 128)] = (grad_k * 0.125).astype(bf16)
+            gpack_s[f, :, lanes(2 * D + 128 * h, 128)] = grad_v.astype(bf16)
+        return carry
+
+    lax.fori_loop(0, H // 2 // GROUP, attend, 0)
+    n, r = norm_parts(time_ref[...].reshape(TILE, D))
+    normed = (n * gain + row_of(vec_ref, S_SHIFT)).astype(bf16)
+    grad_packed = gpack_s[...].reshape(TILE, 3 * D)
+    total[:, : 3 * D] += tn(normed, grad_packed)
+    a = nt(grad_packed, sin_ref[...])
+    time_grad = grad_ref[...].reshape(TILE, D) + norm_back(a, n, r, gain)
+    time_grad_ref[...] = time_grad.reshape(PAIR, ROWS, D)
+    grad_yt = time_grad.astype(bf16)
+    total[:, 4 * D :] += tn(mixed_ref[...].reshape(TILE, D), grad_yt)
+    back_ref[...] = nt(grad_yt, tout_ref[...]).astype(bf16).reshape(PAIR, ROWS, D)
+    sums_ref[0:1] += column_sum(a * n)
+    sums_ref[1:2] += column_sum(a)
+    sums_ref[2:3] += column_sum(grad_ys.astype(f32))
+    sums_ref[3:4] += column_sum(grad_yt.astype(f32))
+    if not first_call:
+
+        @pl.when(step == steps - 1)
+        def _():
+            weights_ref[...] = total[...].astype(bf16)
+
+
+def spatial_backward(which, grad, packed, probs, mixs, time, mixed, vec, second, earlier):
+    slots, mbs, frames = grad.shape[:3]
+
+    def framed(*tail):
+        return pl.BlockSpec(
+            (None, None, PAIR) + tail, lambda m, i: (which, m, i) + (0,) * len(tail)
+        )
+
+    single = pl.BlockSpec((None, PAIR, ROWS, D), lambda m, i: (m, i, 0, 0))
+    scratch = [pltpu.VMEM((PAIR, ROWS, D), bf16), pltpu.VMEM((PAIR, ROWS, 3 * D), bf16)]
+    extra = []
+    if earlier:
+        extra = [pl.BlockSpec(memory_space=pl.ANY), fixed((8, D))]
+        scratch = scratch + [pltpu.VMEM((D, 5 * D), f32)]
+
+    def kernel(*refs):
+        return spatial_backward_kernel(not earlier, *refs)
+
+    return pl.pallas_call(
+        kernel,
+        grid=(mbs, frames // PAIR),
+        in_specs=[
+            framed(ROWS, D),
+            framed(ROWS, 3 * D),
+            framed(H, ROWS, ROWS),
+            framed(ROWS, D),
+            framed(ROWS, D),
+            single,
+            fixed((16, D)),
+            fixed((D, D), (0, 3)),
+            fixed((D, 3 * D)),
+            fixed((D, D), (0, 4)),
+        ]
+        + extra,
+        out_specs=[fixed((D, 5 * D)), fixed((8, D)), single, single],
+        out_shape=[
+            out_of((D, 5 * D), bf16 if earlier else f32),
+            out_of((8, D), f32),
+            out_of((mbs, frames, ROWS, D), f32),
+            out_of((mbs, frames, ROWS, D), bf16),
+        ],
+        scratch_shapes=scratch,
+        compiler_params=pltpu.CompilerParams(vmem_limit_bytes=VMEM_BYTES),
+        cost_estimate=pl.CostEstimate(
+            flops=2 * mbs * frames * ROWS * D * 14 * D, bytes_accessed=60 << 20, transcendentals=0
+        ),
+        name="spatial_backward",
+    )(grad, packed, probs, mixs, time, mixed, vec, second, second, second, *earlier)
+
+
+def temporal_backward_kernel(
+    slot_ref, own_ref, other_ref, packed_ref, probs_ref, back_own_ref, back_other_ref,
+    vec_ref, win_ref, space_sums_ref, mlp_sums_ref, hidden_sums_ref, space_ref,
+    weights_ref, gpack_ref, pad_s, total_s, sums_s, columns_s, copied,
+):
+    m, j = pl.program_id(0), pl.program_id(1)
+    taken = pltpu.make_async_copy(space_ref, weights_ref.at[:, 3 * D + 128 :], copied)
+
+    @pl.when((m == 0) & (j == 0))
+    def _():
+        taken.start()
+        total_s[...] = jnp.zeros_like(total_s)
+        columns_s[...] = jnp.zeros_like(columns_s)
+        sums_s[...] = jnp.zeros_like(sums_s)
+        sums_s[T_BIAS : T_BIAS + 1] = space_sums_ref[3:4]
+        sums_s[S_GAIN : S_GAIN + 3] = space_sums_ref[0:3]
+        sums_s[M_GAIN : M_GAIN + 3] = mlp_sums_ref[0:3]
+        for k in range(CHUNKS):
+            sums_s[HIDDEN + k : HIDDEN + k + 1] = hidden_sums_ref[0:1, k * D : (k + 1) * D]
+        sums_s[16:32] = vec_ref[...]
+        pad_s[...] = jnp.zeros_like(pad_s)
+
+    @pl.when(j < BLOCKS)
+    def _():
+        at = pl.ds(pl.multiple_of(jnp.minimum(j, BLOCKS - 1) * BLOCK, BLOCK), BLOCK)
+
+        def part(h, k):
+            lo = k * D + 128 * h
+            return packed_ref[:, :, lo : lo + 128].reshape(8 * BLOCK, 128)
+
+        def out_pair(h):
+            lo = 128 * h
+            return jnp.concatenate(
+                [back_own_ref[:, :, lo : lo + 128], back_other_ref[:, :, lo : lo + 128]], axis=0
+            ).reshape(8 * BLOCK, 128)
+
+        products = [nt(out_pair(h), stacked(part(h, 2))) for h in range(H // 2)]
+        scores = []
+        for h in range(H // 2):
+            wide = probs_ref[h].astype(f32)
+            product = wide * products[h]
+            pair = []
+            for k in range(2):
+                near = product[:, 128 * k : 128 * k + 128]
+                weight = wide[:, 128 * k : 128 * k + 128]
+                pair.append((near - weight * jnp.sum(near, -1, keepdims=True)).astype(bf16))
+            scores.append(pair)
+        for h in range(H // 2):
+            lo = 128 * h
+            probs = probs_ref[h]
+            grad_v = tn(
+                jnp.concatenate([probs[:, :128], probs[:, 128:]], axis=0), stacked(out_pair(h))
+            )
+            grad_q = nn(jnp.concatenate(scores[h], axis=1), stacked(part(h, 1))) * 0.125
+            grad_k = tn(jnp.concatenate(scores[h], axis=0), stacked(part(h, 0))) * 0.125
+            for k, values_of in enumerate((grad_q, grad_k, grad_v)):
+                gpack_ref[:, at, k * D + lo : k * D + lo + 128] = values_of.astype(bf16).reshape(
+                    8, BLOCK, 128
+                )
+
+    @pl.when(j >= BLOCKS)
+    def _():
+        p = jnp.clip(j - BLOCKS, 0, 1)
+        for f in range(HALF):
+            pad_s[f, :PATCHES] = jnp.where(p == 0, own_ref[f], other_ref[f])
+        n, _ = norm_parts(pad_s[...].reshape(HALF * ROWS, D).astype(f32))
+        grad_packed = gpack_ref[pl.ds(HALF * p, HALF)].reshape(HALF * ROWS, 3 * D)
+        total_s[...] += tn(n.astype(bf16), grad_packed)
+        columns_s[0:1] += column_sum(grad_packed.astype(f32))
+
+    @pl.when((m == pl.num_programs(0) - 1) & (j == pl.num_programs(1) - 1))
+    def _():
+        taken.wait()
+        turned = sums_s[...].T
+        gain, shift = turned[:, 16 + T_GAIN : 17 + T_GAIN], turned[:, 16 + T_SHIFT : 17 + T_SHIFT]
+        g_gain = jnp.zeros((D, 1), f32)
+        g_shift = jnp.zeros((D, 1), f32)
+        for k in range(3):
+            at = slice(k * D, (k + 1) * D)
+            total, columns = total_s[:, at], columns_s[0:1, at]
+            win = win_ref[:, at].astype(f32)
+            weights_ref[:, at] = (gain * total + shift * columns).astype(bf16)
+            g_gain = g_gain + jnp.sum(total * win, -1, keepdims=True)
+            g_shift = g_shift + jnp.sum(columns * win, -1, keepdims=True)
+        lane = lax.broadcasted_iota(jnp.int32, (D, 128), 1)
+        turned = jnp.where(lane == T_GAIN, g_gain, jnp.where(lane == T_SHIFT, g_shift, turned))
+        weights_ref[:, 3 * D : 3 * D + 128] = turned.astype(bf16)
+
+
+def temporal_backward(
+    slot, tokens, other, packed, probs, back_own, back_other, vec, weights,
+    space_sums, mlp_sums, hidden_sums, space,
+):
+    mbs, slots, frames = tokens.shape[:3]
+    def row_block(j):
+        return jnp.minimum(j, BLOCKS - 1)
+
+    rows_of = pl.BlockSpec((None, frames, BLOCK, D), lambda m, j, s: (m, 0, row_block(j), 0))
+    return pl.pallas_call(
+        temporal_backward_kernel,
+        grid_spec=pltpu.PrefetchScalarGridSpec(
+            num_scalar_prefetch=1,
+            grid=(mbs, BLOCKS + 2),
+            in_specs=[
+                pl.BlockSpec((None, None, HALF, PATCHES, D), lambda m, j, s: (m, s[0], 0, 0, 0)),
+                pl.BlockSpec((None, HALF, PATCHES, D), lambda m, j, s: (m, 0, 0, 0)),
+                pl.BlockSpec((None, 8, BLOCK, 3 * D), lambda m, j, s: (m, 0, row_block(j), 0)),
+                pl.BlockSpec(
+                    (None, None, H // 2, 128, 256), lambda m, j, s: (m, row_block(j), 0, 0, 0)
+                ),
+                rows_of,
+                rows_of,
+                fixed((16, D)),
+                fixed((D, 3 * D)),
+                fixed((8, D)),
+                fixed((8, D)),
+                fixed((8, CHUNKS * D)),
+                pl.BlockSpec(memory_space=pl.ANY),
+            ],
+            out_specs=[
+                fixed((D, 8 * D + 128)),
+                pl.BlockSpec((None, 8, ROWS, 3 * D), lambda m, j, s: (m, 0, 0, 0)),
+            ],
+            scratch_shapes=[
+                pltpu.VMEM((HALF, ROWS, D), bf16),
+                pltpu.VMEM((D, 3 * D), f32),
+                pltpu.VMEM((128, D), f32),
+                pltpu.VMEM((8, 3 * D), f32),
+                pltpu.SemaphoreType.DMA(()),
+            ],
+        ),
+        out_shape=[
+            out_of((D, 8 * D + 128), bf16),
+            out_of((mbs, 8, ROWS, 3 * D), bf16),
+        ],
+        compiler_params=pltpu.CompilerParams(vmem_limit_bytes=VMEM_BYTES),
+        cost_estimate=pl.CostEstimate(
+            flops=2 * mbs * 8 * ROWS * D * 5 * D, bytes_accessed=60 << 20, transcendentals=0
+        ),
+        name="temporal_backward",
+    )(
+        slot, tokens, other, packed, probs, back_own, back_other, vec, weights,
+        space_sums, mlp_sums, hidden_sums, space,
+    )
+
+
+def input_grad_kernel(own, *refs):
+    tokens_ref, gpack_ref, vec_ref, win_ref = refs[1:5]
+    out_ref, pad_s = refs[-2:]
+    pad_s[...] = jnp.zeros_like(pad_s)
+    for f in range(PAIR):
+        pad_s[f, :PATCHES] = tokens_ref[f]
+    n, r = norm_parts(pad_s[...].reshape(TILE, D).astype(f32))
+    a = nt(gpack_ref[...].reshape(TILE, 3 * D), win_ref[...])
+    back = norm_back(a, n, r, row_of(vec_ref, T_GAIN)).reshape(PAIR, ROWS, D)
+    if own:
+        back = back + refs[5][...]
+        for f in range(PAIR):
+            out_ref[f] = back[f, :PATCHES].astype(bf16)
+    else:
+        out_ref[...] = back.astype(bf16)
+
+
+def input_grad(own, slot, tokens, gpack, vec, weights, extra, frames):
+    mbs = gpack.shape[0]
+    near = frames // PAIR
+    half = 0 if own else near
+    single = pl.BlockSpec((None, PAIR, ROWS, D), lambda m, i, s: (m, i, 0, 0))
+    outer = pl.BlockSpec((None, None, PAIR, PATCHES, D), lambda m, i, s: (m, s[0], i, 0, 0))
+    other = pl.BlockSpec((None, PAIR, PATCHES, D), lambda m, i, s: (m, i, 0, 0))
+
+    def kernel(*refs):
+        input_grad_kernel(own, *refs)
+
+    return pl.pallas_call(
+        kernel,
+        grid_spec=pltpu.PrefetchScalarGridSpec(
+            num_scalar_prefetch=1,
+            grid=(mbs, near),
+            in_specs=[
+                outer if own else other,
+                pl.BlockSpec((None, PAIR, ROWS, 3 * D), lambda m, i, s: (m, half + i, 0, 0)),
+                fixed((16, D)),
+                fixed((D, 3 * D)),
+            ]
+            + [single] * len(extra),
+            out_specs=outer if own else single,
+            scratch_shapes=[pltpu.VMEM((PAIR, ROWS, D), bf16)],
+        ),
+        out_shape=out_of(tokens.shape if own else (mbs, frames, ROWS, D), bf16),
+        compiler_params=pltpu.CompilerParams(vmem_limit_bytes=VMEM_BYTES),
+        cost_estimate=pl.CostEstimate(
+            flops=2 * mbs * frames * ROWS * D * 3 * D, bytes_accessed=20 << 20, transcendentals=0
+        ),
+        name="input_grad",
+    )(slot, tokens, gpack, vec, weights, *extra)
+
+
+def last_sum_kernel(slot_ref, time_grad_ref, back_ref, patch_in_ref, patch_ref):
+    del patch_in_ref
+    whole = time_grad_ref[...] + back_ref[...].astype(f32)
+    for f in range(PAIR):
+        patch_ref[f] = whole[f, :PATCHES].astype(bf16)
+
+
+def last_sum(slot, time_grad, back, patch):
+    mbs, frames = time_grad.shape[:2]
+    single = pl.BlockSpec((None, PAIR, ROWS, D), lambda m, i, s: (m, i, 0, 0))
+    return pl.pallas_call(
+        last_sum_kernel,
+        grid_spec=pltpu.PrefetchScalarGridSpec(
+            num_scalar_prefetch=1,
+            grid=(mbs, frames // PAIR),
+            in_specs=[single, single, pl.BlockSpec(memory_space=pl.ANY)],
+            out_specs=pl.BlockSpec(
+                (None, None, PAIR, PATCHES, D), lambda m, i, s: (m, s[1], i, 0, 0)
+            ),
+        ),
+        out_shape=out_of(patch.shape, bf16),
+        input_output_aliases={3: 0},
+        name="last_sum",
+    )(slot, time_grad, back, patch)
+
+
+AXES = ("clip", "frame")
+
+
+def swap(values):
+    return lax.ppermute(values, "frame", [(0, 1), (1, 0)])
+
+
+def gather(values):
+    return lax.all_gather(values, AXES, axis=0, tiled=True)
+
+
+def scatter_sum(values):
+    return lax.psum_scatter(values, AXES, scatter_dimension=0, tiled=True)
+
+
+def paired_body(
+    patch_tokens, live_slots, out_grad,
+    temporal_gain, temporal_shift, temporal_in, temporal_out, temporal_bias,
+    spatial_gain, spatial_shift, spatial_in, spatial_out, spatial_bias,
+    mlp_gain, mlp_shift, expand_weight, expand_bias, shrink_weight, shrink_bias,
+):
+    rows = temporal_in.shape[0]
+    mine = lax.axis_index("frame")
+    slot = jnp.stack([mine, 1 - mine]).astype(jnp.int32)
+    sent = lax.dynamic_index_in_dim(patch_tokens, 1 - mine, 1, keepdims=False)
+    other = swap(sent)
+
+    columns = [
+        v[:, None]
+        for v in (
+            temporal_gain, temporal_shift, temporal_bias, spatial_gain, spatial_shift,
+            spatial_bias, mlp_gain, mlp_shift, shrink_bias,
+        )
+    ] + [expand_bias.reshape(rows, CHUNKS)]
+    columns = jnp.concatenate(columns, axis=1)
+    columns = jnp.pad(columns, ((0, 0), (0, 128 - columns.shape[1])))
+    first = gather(jnp.concatenate([temporal_in, columns], axis=1))
+    second = gather(jnp.concatenate([spatial_in, temporal_out, spatial_out], axis=1))
+    turned = expand_weight.reshape(rows, D, CHUNKS).transpose(0, 2, 1).reshape(rows, CHUNKS * D)
+    third = gather(
+        jnp.concatenate([turned, shrink_weight.reshape(rows, CHUNKS * D)], axis=1)
+    )
+    vec = first[:, 3 * D :].T[:16].astype(f32)
+    hidden = vec[HIDDEN : HIDDEN + CHUNKS].reshape(1, CHUNKS * D)
+
+    mbs, frames = patch_tokens.shape[0], patch_tokens.shape[2]
+    packed_t, probs_t, mixed_own, mixed_other = temporal_forward(
+        slot, patch_tokens, other, vec, first
+    )
+    mixed_here = swap(mixed_other)
+    saved = spatial_forward(0, slot, patch_tokens, mixed_own, vec, second, ())
+    saved = spatial_forward(1, slot, patch_tokens, mixed_here, vec, second, saved)
+    time, packed_s, probs_s, mixed_s, space = saved
+
+    live = (slot[:, None] < live_slots[:, 0][None, :]).astype(jnp.int32)
+    live = jnp.repeat(live.reshape(-1), frames // PAIR)
+    block_out, space_grad, g_mlp, sums_m, sums_h = mlp(
+        slot, live, space, out_grad, vec, hidden, third
+    )
+    g_mlp = scatter_sum(g_mlp)
+
+    kept = (space_grad, packed_s, probs_s, mixed_s, time)
+    g_far, sums_s, time_grad_far, back_far = spatial_backward(
+        1, *kept, mixed_here, vec, second, ()
+    )
+    back_other = swap(back_far)
+    g_space, sums_s, time_grad_own, back_own = spatial_backward(
+        0, *kept, mixed_own, vec, second, (g_far, sums_s)
+    )
+    g_rest, gpack = temporal_backward(
+        slot, patch_tokens, other, packed_t, probs_t, back_own, back_other, vec, first,
+        sums_s, sums_m, sums_h, g_space,
+    )
+    g_rest, g_mlp = lax.optimization_barrier((g_rest, g_mlp))
+    g_rest = scatter_sum(g_rest)
+    send = input_grad(False, slot, other, gpack, vec, first, (), frames)
+    patch_grad = input_grad(
+        True, slot, patch_tokens, gpack, vec, first, (time_grad_own,), frames
+    )
+    patch_grad = last_sum(slot, time_grad_far, swap(send), patch_grad)
+
+    g_rest, g_mlp = g_rest.astype(f32), g_mlp.astype(f32)
+    tail, g_space = g_rest[:, 3 * D : 3 * D + 128], g_rest[:, 3 * D + 128 :]
+
+    def vector(at):
+        return tail[:, at]
+
+    wide = CHUNKS * D
+    g_expand = g_mlp[:, :wide].reshape(rows, CHUNKS, D).transpose(0, 2, 1).reshape(rows, wide)
+    return (
+        block_out,
+        patch_grad,
+        vector(T_GAIN),
+        vector(T_SHIFT),
+        g_rest[:, : 3 * D],
+        g_space[:, 4 * D :],
+        vector(T_BIAS),
+        vector(S_GAIN),
+        vector(S_SHIFT),
+        g_space[:, : 3 * D],
+        g_space[:, 3 * D : 4 * D],
+        vector(S_BIAS),
+        vector(M_GAIN),
+        vector(M_SHIFT),
+        g_expand,
+        tail[:, HIDDEN : HIDDEN + CHUNKS].reshape(rows * CHUNKS),
+        g_mlp[:, wide:].reshape(rows * CHUNKS, D),
+        vector(M_BIAS),
+    )
+
+
+def body(*args):
+    tokens, temporal_in, expand_weight = args[0], args[5], args[15]
+    paired = (
+        lax.axis_size("frame") == 2
+        and tokens.shape[1:] == (2, 4, PATCHES, D)
+        and temporal_in.shape[1] == 3 * D
+        and expand_weight.shape[1] == CHUNKS * CHUNK
+    )
+    return paired_body(*args) if paired else generic_body(*args)
+
+
 def solution(mesh):
     placed = (
         P(None, "clip", "frame", None, None),

time: 2770 us -> 758 us (0.27)
  waiting for transfers between devices: 1020 us -> 209 us
  matrix products: 738 us -> 0 us
  local copies, waits for them, and re-layouts: 611 us -> 47.6 us
  Pallas kernels: 0 us -> 464 us
  other arithmetic: 190 us -> 5.61 us
  blocking collectives: 122 us -> 0 us
  starting transfers between devices: 49 us -> 7.11 us
    dot_general x60 -> x0, matrix products: 738 us -> none  [the longest x12 203 us: forward_dot(): return jnp.dot(left, right, preferred_element_type=jnp.float32)]
    reduce_scatter x6 -> x1, waiting for transfers between devices: 690 us -> 0.02 us  [scatter_sum(): return lax.psum_scatter(values, AXES, scatter_dimension=0, tiled=True)]
    pallas_call x0 -> x10, Pallas kernels: none -> 464 us  [the longest x1 146 us: mlp(): pl.pallas_call(mlp_kernel, grid_spec=pltpu.PrefetchScalarGridSpec(num_sca...]
    all_to_all x8 -> x0, waiting for transfers between devices: 323 us -> none  [the longest x2 158 us: micro_batch(): lax.all_to_all(to_patch_rows(packed_t, slot_count, local_frames, patch_co...]
    reshape x32 -> x7, local copies, waits for them, and re-layouts: 243 us -> 4.61 us  [the longest x1 1.01 us: paired_body(): shrink_weight.reshape(rows, CHUNKS * D)]
    ppermute x0 -> x4, waiting for transfers between devices: none -> 135 us  [swap(): return lax.ppermute(values, 'frame', [(0, 1), (1, 0)])]
    while x366 -> x0, local copies, waits for them, and re-layouts: 108 us -> none
    convert_element_type x16 -> x2, local copies, waits for them, and re-layouts: 91.3 us -> 0.84 us  [the longest x1 0.76 us: paired_body(): vec = first[:, 3 * D:].T[:16].astype(f32)]
  transfers between devices with their start and end apart: 26 -> 9, of which waited for: 15 -> 7; matrix products, arithmetic and copies ran while one was open for 29% -> 5% of each run, Pallas kernels for 0% -> 43%
where the time goes in v1:
time: 758 us; the launch traced here: 748 us
  Pallas kernels  464 us (61%)
  waiting for transfers between devices  209 us (28%)
  local copies, waits for them, and re-layouts  47.6 us (6%)
  between operations  14.4 us (2%)
    pallas_call x1, Pallas kernels, mlp(): pl.pallas_call(mlp_kernel, grid_spec=pltpu.PrefetchScalarGridSpec(num_sca...  146 us
    ppermute x4, waiting for transfers between devices, swap(): return lax.ppermute(values, 'frame', [(0, 1), (1, 0)])  135 us
    pallas_call x2, Pallas kernels, spatial_backward(): pl.pallas_call(kernel, grid=(mbs, frames // PAIR), in_specs=[framed(ROWS,...  116 us
    pallas_call x1, Pallas kernels, temporal_backward(): pl.pallas_call(temporal_backward_kernel, grid_spec=pltpu.PrefetchScalarGr...  62.4 us
    pallas_call x2, Pallas kernels, spatial_forward(): pl.pallas_call(spatial_forward_kernel, grid_spec=pltpu.PrefetchScalarGrid...  61.7 us
    pallas_call x1, Pallas kernels, temporal_forward(): pl.pallas_call(temporal_forward_kernel, grid_spec=pltpu.PrefetchScalarGri...  45.2 us
    unnamed x6, waiting for transfers between devices  44.4 us
    all_gather x3, waiting for transfers between devices, gather(): return lax.all_gather(values, AXES, axis=0, tiled=True)  29.4 us
  transfers between devices with their start and end apart: 9, of which 7 were waited for; matrix products, arithmetic and copies ran while one was open for 5% of the time, Pallas kernels for 43%

profile of v1, /device:TPU:0, one launch (start us, length us, event | category | flops | bytes accessed | tf_op | source)
XLA Modules:
  0.0 748.1 jit_solution(6974879157023193626)
XLA Ops:
  21.9 2.7 dynamic-slice_bitcast_fusion
  24.5 3.0 collective-permute-start
  27.6 2.8 copy.152.own_ref.refs_1_
  30.9 59.8 %collective-permute-done = bf16[2,4,196,768]{3,1,2,0:T(4,128)(2,1)S(1)} collective-permute-done((bf16[2,4,196,768]{3,1,2,0:T(4,128)(2,1)S(1)}, bf16[2,4,196,768]{3,1,2,0:T(4,128)(2,1)S(1)}, u32[]{:S(2)}, u32[]{:S(2)}) %collective-permute-start) | collective-permute-done | bytes 2408480 | tf_op jit(solution)/shard_map/ppermute | solution.py:1130
  94.2 45.2 %temporal_forward.1 = (bf16[2,8,208,2304]{3,2,1,0:T(8,128)(2,1)}, bf16[2,13,6,128,256]{4,3,2,1,0:T(8,128)(2,1)}, bf16[2,4,208,768]{3,2,1,0:T(8,128)(2,1)}, bf16[2,4,208,768]{3,2,1,0:T(8,128)(2,1)}) custom-call(s32[2]{0:T(128)} %pad_add_fusion.slot_ref.refs_0_, bf16[2,2,4,196,768]{4,3,2,1,0:T(8,128)(2,1)} %copy.152.own_ref.refs_1_, ...), custom_call_target="tpu_custom_call" | custom-call | flops 15703474176 | bytes 62914560 | tf_op jit(solution)/shard_map/temporal_forward/pallas_call | solution.py:510
  139.3 1.8 collective-permute-start.1
  141.9 5.2 copy.157.cotan_ref
  148.1 16.2 %all-gather.6.cloned.1.call-done.refs_4_.refs_5_.refs_6_.refs_7_.refs_8_.refs_9_ = bf16[768,3840]{1,0:T(8,128)(2,1)} async-done(((bf16[24,3840]{1,0:T(8,128)(2,1)}), bf16[768,3840]{1,0:T(8,128)(2,1)}) %all-gather.6.cloned.1.call-update) | async-done | bytes 5898256 | tf_op jit(solution)/shard_map/all_gather | solution.py:1134
  164.3 30.8 %spatial_forward.2 = (f32[2,2,4,208,768]{4,3,2,1,0:T(8,128)}, bf16[2,2,4,208,2304]{4,3,2,1,0:T(8,128)(2,1)}, bf16[2,2,4,12,208,208]{5,4,3,2,1,0:T(8,128)(2,1)}, ...) custom-call(s32[2]{0:T(128)} %pad_add_fusion.slot_ref.refs_0_, ...), custom_call_target="tpu_custom_call" | custom-call | flops 11777605632 | bytes 62914560 | tf_op jit(solution)/shard_map/spatial_forward/pallas_call | solution.py:604
  195.1 18.8 %collective-permute-done.1.refs_2_.refs_5_ = bf16[2,4,208,768]{3,2,1,0:T(8,128)(2,1)} collective-permute-done((bf16[2,4,208,768]{3,2,1,0:T(8,128)(2,1)}, bf16[2,4,208,768]{3,2,1,0:T(8,128)(2,1)}, u32[]{:S(2)}, u32[]{:S(2)}) %collective-permute-start.1) | collective-permute-done | bytes 2555936 | tf_op jit(solution)/shard_map/ppermute | solution.py:1130
  213.9 31.0 %spatial_forward.3 = (f32[2,2,4,208,768]{4,3,2,1,0:T(8,128)}, bf16[2,2,4,208,2304]{4,3,2,1,0:T(8,128)(2,1)}, bf16[2,2,4,12,208,208]{5,4,3,2,1,0:T(8,128)(2,1)}, ...) custom-call(s32[2]{0:T(128)} %pad_add_fusion.slot_ref.refs_0_, ...), custom_call_target="tpu_custom_call", output_to_operand_aliasing={{0}: (7, {}), {1}: (8, {}), {2}: (9, {}), {3}: (10, {}), {4... | custom-call | flops 11777605632 | bytes 62914560 | tf_op jit(solution)/shard_map/spatial_forward/pallas_call | solution.py:604
  244.9 13.2 %all-gather.8.cloned.1.call-done.expand_ref.shrink_ref = bf16[768,6144]{1,0:T(8,128)(2,1)} async-done(((bf16[24,6144]{1,0:T(8,128)(2,1)}), bf16[768,6144]{1,0:T(8,128)(2,1)}) %all-gather.8.cloned.1.call-update) | async-done | bytes 9437200 | tf_op jit(solution)/shard_map/all_gather | solution.py:1134
  258.0 145.9 %mlp.1 = (bf16[2,2,4,196,768]{4,3,2,1,0:T(8,128)(2,1)}, f32[2,2,4,208,768]{4,3,2,1,0:T(8,128)}, bf16[768,6144]{1,0:T(8,128)(2,1)}, f32[8,768]{1,0:T(8,128)}, f32[8,3072]{1,0:T(8,128)}) custom-call(s32[2]{0:T(128)} %pad_add_fusion.slot_ref.refs_0_, s32[8]{0:T(128)} %reshape.74.live_ref, f32[2,2,4,208,768]{4,3,2,1,0:T(8,128)} %get-tuple-element.56.space_ref, ...), custom_call_target="tpu_custom_call" | custom-call | flops 94220845056 | bytes 62914560 | tf_op jit(solution)/shard_map/mlp/pallas_call | solution.py:727
  404.0 55.6 %spatial_backward.2 = (f32[768,3840]{1,0:T(8,128)}, f32[8,768]{1,0:T(8,128)}, f32[2,4,208,768]{3,2,1,0:T(8,128)}, bf16[2,4,208,768]{3,2,1,0:T(8,128)(2,1)}) custom-call(f32[2,2,4,208,768]{4,3,2,1,0:T(8,128)} %get-tuple-element.58.refs_0_, bf16[2,2,4,208,2304]{4,3,2,1,0:T(8,128)(2,1)} %get-tuple-element.59.refs_1_, ...), custom_call_target="tpu_custom_call" | custom-call | flops 27481079808 | bytes 62914560 | tf_op jit(solution)/shard_map/spatial_backward/pallas_call | solution.py:870
  461.1 60.0 %spatial_backward.3 = (bf16[768,3840]{1,0:T(8,128)(2,1)}, f32[8,768]{1,0:T(8,128)}, f32[2,4,208,768]{3,2,1,0:T(8,128)}, bf16[2,4,208,768]{3,2,1,0:T(8,128)(2,1)}) custom-call(f32[2,2,4,208,768]{4,3,2,1,0:T(8,128)} %get-tuple-element.58.refs_0_, bf16[2,2,4,208,2304]{4,3,2,1,0:T(8,128)(2,1)} %get-tuple-element.59.refs_1_, ...), custom_call_target="tpu_custom_call" | custom-call | flops 27481079808 | bytes 62914560 | tf_op jit(solution)/shard_map/spatial_backward/pallas_call | solution.py:870
  521.1 11.5 %collective-permute-done.2.back_other_ref = bf16[2,4,208,768]{3,2,1,0:T(8,128)(2,1)} collective-permute-done((bf16[2,4,208,768]{3,2,1,0:T(8,128)(2,1)}, bf16[2,4,208,768]{3,2,1,0:T(8,128)(2,1)}, u32[]{:S(2)}, u32[]{:S(2)}) %collective-permute-start.2) | collective-permute-done | bytes 2555936 | tf_op jit(solution)/shard_map/ppermute | solution.py:1130
  532.6 62.4 %temporal_backward.1 = (bf16[768,6272]{1,0:T(8,128)(2,1)}, bf16[2,8,208,2304]{3,2,1,0:T(8,128)(2,1)}) custom-call(s32[2]{0:T(128)} %pad_add_fusion.slot_ref.refs_0_, bf16[2,2,4,196,768]{4,3,2,1,0:T(8,128)(2,1)} %copy.152.own_ref.refs_1_, bf16[2,4,196,768]{3,2,1,0:T(8,128)(2,1)} %copy.148.other_ref.refs_1_, ...), custom_call_target="tpu_custom_call" | custom-call | flops 19629342720 | bytes 62914560 | tf_op jit(solution)/shard_map/temporal_backward/pallas_call | solution.py:1000
  595.0 12.6 %input_grad.2 = bf16[2,4,208,768]{3,2,1,0:T(8,128)(2,1)} custom-call(s32[2]{0:T(128)} %pad_add_fusion.slot_ref.refs_0_, bf16[2,4,196,768]{3,2,1,0:T(8,128)(2,1)} %copy.148.other_ref.refs_1_, bf16[2,8,208,2304]{3,2,1,0:T(8,128)(2,1)} %get-tuple-element.74.refs_2_, f32[16,768]{1,0:T(8,128)} %copy.149.vec_ref.refs_3_.refs_6_, ...), custom_call_target="tpu_custom_call" | custom-call | flops 5888802816 | bytes 20971520 | tf_op jit(solution)/shard_map/input_grad/pallas_call | solution.py:1076
  608.3 6.7 copy.169
  615.0 15.1 %input_grad.3.patch_in_ref = bf16[2,2,4,196,768]{4,3,2,1,0:T(8,128)(2,1)} custom-call(s32[2]{0:T(128)} %pad_add_fusion.slot_ref.refs_0_, bf16[2,2,4,196,768]{4,3,2,1,0:T(8,128)(2,1)} %copy.152.own_ref.refs_1_, bf16[2,8,208,2304]{3,2,1,0:T(8,128)(2,1)} %get-tuple-element.74.refs_2_, f32[16,768]{1,0:T(8,128)} %copy.149.vec_ref.refs_3_.refs_6_, ...), custom_call_target="tpu_custom_call" | custom-call | flops 5888802816 | bytes 20971520 | tf_op jit(solution)/shard_map/input_grad/pallas_call | solution.py:1076
  630.1 45.1 %collective-permute-done.3.back_ref = bf16[2,4,208,768]{3,2,1,0:T(8,128)(2,1)} collective-permute-done((bf16[2,4,208,768]{3,2,1,0:T(8,128)(2,1)}, bf16[2,4,208,768]{3,2,1,0:T(8,128)(2,1)}, u32[]{:S(2)}, u32[]{:S(2)}) %collective-permute-start.3) | collective-permute-done | bytes 2555936 | tf_op jit(solution)/shard_map/ppermute | solution.py:1130
  675.1 5.9 last_sum.1
  681.0 6.5 copy.170
  690.4 44.3 %reduce-scatter.7.cloned.1.call-done = bf16[24,6272]{1,0:T(8,128)(2,1)} async-done(((bf16[768,6272]{1,0:T(8,128)(2,1)}), bf16[24,6272]{1,0:T(8,128)(2,1)}) %reduce-scatter.7.cloned.1.call-update) | async-done | bytes 301072
  (63 shorter events, 31.8 us)
Async XLA Ops:
  7.2 85.2 %all-gather.4.cloned.1.call-start = ((), (), s32[]{:S(2)}) async-start(), calls=%async_computation.2 | async-start | bytes 3852288 | tf_op jit(solution)/shard_map/all_gather | solution.py:1134
  16.4 147.9 %all-gather.6.cloned.1.call-start = ((), (), s32[]{:S(2)}) async-start(), calls=%async_computation.3 | async-start | bytes 6082560 | tf_op jit(solution)/shard_map/all_gather | solution.py:1134
  18.1 239.9 %all-gather.8.cloned.1.call-start = ((), (), s32[]{:S(2)}) async-start(), calls=%async_computation.4 | async-start | bytes 9732096 | tf_op jit(solution)/shard_map/all_gather | solution.py:1134
  21.8 573.2 %reduce-scatter.5.cloned.1.call-start = ((), (), s32[]{:S(2)}) async-start(), calls=%async_computation.5 | async-start | bytes 9732096 | tf_op jit(solution)/shard_map/reduce_scatter | solution.py:1138
  21.8 5.7 copy-start
  24.5 66.2 %collective-permute-start = (bf16[2,4,196,768]{3,1,2,0:T(4,128)(2,1)S(1)}, bf16[2,4,196,768]{3,1,2,0:T(4,128)(2,1)S(1)}, u32[]{:S(2)}, u32[]{:S(2)}) collective-permute-start(bf16[2,4,196,768]{3,1,2,0:T(4,128)(2,1)S(1)} %dynamic-slice_bitcast_fusion), channel_id=1, source_target_pairs={{0,1},{1,0},{2,3},{3,2},{4,5},{5,4},{6,7},{7,6},{8,9},{9,8},{10,11... | collective-permute-start | bytes 7225352 | tf_op jit(solution)/shard_map/ppermute | solution.py:1130
  94.2 46.9 %copy-start.2 = (s32[2]{0:T(128)S(1)}, s32[2]{0:T(128)}, u32[]{:S(2)}) copy-start(s32[2]{0:T(128)} %pad_add_fusion.slot_ref.refs_0_) | copy-start | bytes 28
  94.2 46.9 %copy-start.3 = (s32[2,1]{0,1:T(1,128)S(1)}, s32[2,1]{0,1:T(1,128)}, u32[]{:S(2)}) copy-start(s32[2,1]{0,1:T(1,128)} %param.20) | copy-start | bytes 28
  139.3 74.6 %collective-permute-start.1 = (bf16[2,4,208,768]{3,2,1,0:T(8,128)(2,1)}, bf16[2,4,208,768]{3,2,1,0:T(8,128)(2,1)}, u32[]{:S(2)}, u32[]{:S(2)}) collective-permute-start(bf16[2,4,208,768]{3,2,1,0:T(8,128)(2,1)} %get-tuple-element.49), channel_id=1, source_target_pairs={{0,1},{1,0},{2,3},{3,2},{4,5},{5,4},{6,7},{7,6},{8,9},{9,8},{10,11... | collective-permute-start | bytes 7667720 | tf_op jit(solution)/shard_map/ppermute | solution.py:1130
  404.0 330.7 %reduce-scatter.7.cloned.1.call-start = ((), (), s32[]{:S(2)}) async-start(), calls=%async_computation.6 | async-start | bytes 9934848
  459.6 72.9 %collective-permute-start.2 = (bf16[2,4,208,768]{3,2,1,0:T(8,128)(2,1)}, bf16[2,4,208,768]{3,2,1,0:T(8,128)(2,1)}, u32[]{:S(2)}, u32[]{:S(2)}) collective-permute-start(bf16[2,4,208,768]{3,2,1,0:T(8,128)(2,1)} %get-tuple-element.69), channel_id=1, source_target_pairs={{0,1},{1,0},{2,3},{3,2},{4,5},{5,4},{6,7},{7,6},{8,9},{9,8},{10,11... | collective-permute-start | bytes 7667720 | tf_op jit(solution)/shard_map/ppermute | solution.py:1130
  607.7 67.5 %collective-permute-start.3 = (bf16[2,4,208,768]{3,2,1,0:T(8,128)(2,1)}, bf16[2,4,208,768]{3,2,1,0:T(8,128)(2,1)}, u32[]{:S(2)}, u32[]{:S(2)}) collective-permute-start(bf16[2,4,208,768]{3,2,1,0:T(8,128)(2,1)} %input_grad.2), channel_id=1, source_target_pairs={{0,1},{1,0},{2,3},{3,2},{4,5},{5,4},{6,7},{7,6},{8,9},{9,8},{10,11... | collective-permute-start | bytes 7667720 | tf_op jit(solution)/shard_map/ppermute | solution.py:1130
  681.0 6.5 copy-start.1
Sparse Core Ops, SparseCore 0:
  16.5 72.0 all-gather.3
  92.1 72.1 all-gather.5
  167.8 90.1 all-gather.7
  404.1 143.7 reduce-scatter.4
  595.1 139.5 reduce-scatter.6

commit v2 on v1

--- a/solution.py
+++ b/solution.py
@@ -14,6 +14,7 @@
 HALF = 4
 TILE = PAIR * ROWS
 GROUP = 3
+BACK_GROUP = 6
 CHUNK = 768
 CHUNKS = 4
 BLOCK = 16
@@ -775,11 +776,11 @@
     ) = refs[:10]
     if first_call:
         weights_ref, sums_ref, time_grad_ref, back_ref, gmix_s, gpack_s = refs[-6:]
-        in_acc = out_acc = tail_acc = None
         total = weights_ref
     else:
         total_ref, sums_before_ref = refs[10:12]
-        weights_ref, sums_ref, time_grad_ref, back_ref, gmix_s, gpack_s, total = refs[-7:]
+        weights_ref, sums_ref, time_grad_ref, back_ref, gmix_s, gpack_s, total, copied = refs[-8:]
+        taken = pltpu.make_async_copy(total_ref, total, copied)
     step = pl.program_id(0) * pl.num_programs(1) + pl.program_id(1)
     steps = pl.num_programs(0) * pl.num_programs(1)
 
@@ -789,17 +790,16 @@
             total[...] = jnp.zeros_like(total)
             sums_ref[...] = jnp.zeros_like(sums_ref)
         else:
-            pltpu.sync_copy(total_ref, total)
+            taken.start()
             sums_ref[...] = sums_before_ref[...]
 
     gain = row_of(vec_ref, S_GAIN)
     space_grad = grad_ref[...].reshape(TILE, D)
     grad_ys = space_grad.astype(bf16)
-    total[:, 3 * D : 4 * D] += tn(mixs_ref[...].reshape(TILE, D), grad_ys)
     gmix_s[...] = nt(grad_ys, sout_ref[...]).astype(bf16).reshape(PAIR, ROWS, D)
 
     def attend(g, carry):
-        both = [(f, GROUP * g + i) for i in range(GROUP) for f in range(PAIR)]
+        both = [(f, BACK_GROUP * g + i) for i in range(BACK_GROUP) for f in range(PAIR)]
 
         def part(f, h, k):
             return packed_ref[f, :, lanes(k * D + 128 * h, 128)]
@@ -827,7 +827,10 @@
             gpack_s[f, :, lanes(2 * D + 128 * h, 128)] = grad_v.astype(bf16)
         return carry
 
-    lax.fori_loop(0, H // 2 // GROUP, attend, 0)
+    lax.fori_loop(0, H // 2 // BACK_GROUP, attend, 0)
+    if not first_call:
+        pl.when(step == 0)(taken.wait)
+    total[:, 3 * D : 4 * D] += tn(mixs_ref[...].reshape(TILE, D), grad_ys)
     n, r = norm_parts(time_ref[...].reshape(TILE, D))
     normed = (n * gain + row_of(vec_ref, S_SHIFT)).astype(bf16)
     grad_packed = gpack_s[...].reshape(TILE, 3 * D)
@@ -862,7 +865,7 @@
     extra = []
     if earlier:
         extra = [pl.BlockSpec(memory_space=pl.ANY), fixed((8, D))]
-        scratch = scratch + [pltpu.VMEM((D, 5 * D), f32)]
+        scratch = scratch + [pltpu.VMEM((D, 5 * D), f32), pltpu.SemaphoreType.DMA(())]
 
     def kernel(*refs):
         return spatial_backward_kernel(not earlier, *refs)

time: 758 us -> 758 us (level)
  Pallas kernels: 464 us -> 454 us
  waiting for transfers between devices: 209 us -> 219 us
    pallas_call x2, Pallas kernels: 116 us -> 105 us  [spatial_backward(): pl.pallas_call(kernel, grid=(mbs, frames // PAIR), in_specs=[framed(ROWS,...]
    ppermute x4, waiting for transfers between devices: 135 us -> 145 us  [swap(): return lax.ppermute(values, 'frame', [(0, 1), (1, 0)])]
  transfers between devices with their start and end apart: 9 -> 9, of which waited for: 7 -> 7; matrix products, arithmetic and copies ran while one was open for 5% -> 5% of each run, Pallas kernels for 43% -> 41%
where the time goes in v2:
time: 758 us; the launch traced here: 747 us
  Pallas kernels  454 us (60%)
  waiting for transfers between devices  219 us (29%)
  local copies, waits for them, and re-layouts  47.7 us (6%)
  between operations  14.1 us (2%)
    ppermute x4, waiting for transfers between devices, swap(): return lax.ppermute(values, 'frame', [(0, 1), (1, 0)])  145 us
    pallas_call x1, Pallas kernels, mlp(): pl.pallas_call(mlp_kernel, grid_spec=pltpu.PrefetchScalarGridSpec(num_sca...  145 us
    pallas_call x2, Pallas kernels, spatial_backward(): pl.pallas_call(kernel, grid=(mbs, frames // PAIR), in_specs=[framed(ROWS,...  105 us
    pallas_call x1, Pallas kernels, temporal_backward(): pl.pallas_call(temporal_backward_kernel, grid_spec=pltpu.PrefetchScalarGr...  62.6 us
    pallas_call x2, Pallas kernels, spatial_forward(): pl.pallas_call(spatial_forward_kernel, grid_spec=pltpu.PrefetchScalarGrid...  61.9 us
    pallas_call x1, Pallas kernels, temporal_forward(): pl.pallas_call(temporal_forward_kernel, grid_spec=pltpu.PrefetchScalarGri...  45.2 us
    unnamed x6, waiting for transfers between devices  44.4 us
    all_gather x3, waiting for transfers between devices, gather(): return lax.all_gather(values, AXES, axis=0, tiled=True)  29.3 us
  transfers between devices with their start and end apart: 9, of which 7 were waited for; matrix products, arithmetic and copies ran while one was open for 5% of the time, Pallas kernels for 41%

profile of v2, /device:TPU:0, one launch (start us, length us, event | category | flops | bytes accessed | tf_op | source)
XLA Modules:
  0.0 747.4 jit_solution(11769655204568237331)
XLA Ops:
  21.9 2.7 dynamic-slice_bitcast_fusion
  24.5 3.0 collective-permute-start
  27.6 2.8 copy.152.own_ref.refs_1_
  30.9 59.8 %collective-permute-done = bf16[2,4,196,768]{3,1,2,0:T(4,128)(2,1)S(1)} collective-permute-done((bf16[2,4,196,768]{3,1,2,0:T(4,128)(2,1)S(1)}, bf16[2,4,196,768]{3,1,2,0:T(4,128)(2,1)S(1)}, u32[]{:S(2)}, u32[]{:S(2)}) %collective-permute-start) | collective-permute-done | bytes 2408480 | tf_op jit(solution)/shard_map/ppermute | solution.py:1133
  94.2 45.2 %temporal_forward.1 = (bf16[2,8,208,2304]{3,2,1,0:T(8,128)(2,1)}, bf16[2,13,6,128,256]{4,3,2,1,0:T(8,128)(2,1)}, bf16[2,4,208,768]{3,2,1,0:T(8,128)(2,1)}, bf16[2,4,208,768]{3,2,1,0:T(8,128)(2,1)}) custom-call(s32[2]{0:T(128)} %pad_add_fusion.slot_ref.refs_0_, bf16[2,2,4,196,768]{4,3,2,1,0:T(8,128)(2,1)} %copy.152.own_ref.refs_1_, ...), custom_call_target="tpu_custom_call" | custom-call | flops 15703474176 | bytes 62914560 | tf_op jit(solution)/shard_map/temporal_forward/pallas_call | solution.py:511
  139.3 1.8 collective-permute-start.1
  141.9 5.2 copy.157.cotan_ref
  148.1 16.2 %all-gather.6.cloned.1.call-done.refs_4_.refs_5_.refs_6_.refs_7_.refs_8_.refs_9_ = bf16[768,3840]{1,0:T(8,128)(2,1)} async-done(((bf16[24,3840]{1,0:T(8,128)(2,1)}), bf16[768,3840]{1,0:T(8,128)(2,1)}) %all-gather.6.cloned.1.call-update) | async-done | bytes 5898256 | tf_op jit(solution)/shard_map/all_gather | solution.py:1137
  164.3 30.8 %spatial_forward.2 = (f32[2,2,4,208,768]{4,3,2,1,0:T(8,128)}, bf16[2,2,4,208,2304]{4,3,2,1,0:T(8,128)(2,1)}, bf16[2,2,4,12,208,208]{5,4,3,2,1,0:T(8,128)(2,1)}, ...) custom-call(s32[2]{0:T(128)} %pad_add_fusion.slot_ref.refs_0_, ...), custom_call_target="tpu_custom_call" | custom-call | flops 11777605632 | bytes 62914560 | tf_op jit(solution)/shard_map/spatial_forward/pallas_call | solution.py:605
  195.1 18.8 %collective-permute-done.1.refs_2_.refs_5_ = bf16[2,4,208,768]{3,2,1,0:T(8,128)(2,1)} collective-permute-done((bf16[2,4,208,768]{3,2,1,0:T(8,128)(2,1)}, bf16[2,4,208,768]{3,2,1,0:T(8,128)(2,1)}, u32[]{:S(2)}, u32[]{:S(2)}) %collective-permute-start.1) | collective-permute-done | bytes 2555936 | tf_op jit(solution)/shard_map/ppermute | solution.py:1133
  213.9 31.1 %spatial_forward.3 = (f32[2,2,4,208,768]{4,3,2,1,0:T(8,128)}, bf16[2,2,4,208,2304]{4,3,2,1,0:T(8,128)(2,1)}, bf16[2,2,4,12,208,208]{5,4,3,2,1,0:T(8,128)(2,1)}, ...) custom-call(s32[2]{0:T(128)} %pad_add_fusion.slot_ref.refs_0_, ...), custom_call_target="tpu_custom_call", output_to_operand_aliasing={{0}: (7, {}), {1}: (8, {}), {2}: (9, {}), {3}: (10, {}), {4... | custom-call | flops 11777605632 | bytes 62914560 | tf_op jit(solution)/shard_map/spatial_forward/pallas_call | solution.py:605
  245.0 13.1 %all-gather.8.cloned.1.call-done.expand_ref.shrink_ref = bf16[768,6144]{1,0:T(8,128)(2,1)} async-done(((bf16[24,6144]{1,0:T(8,128)(2,1)}), bf16[768,6144]{1,0:T(8,128)(2,1)}) %all-gather.8.cloned.1.call-update) | async-done | bytes 9437200 | tf_op jit(solution)/shard_map/all_gather | solution.py:1137
  258.1 145.5 %mlp.1 = (bf16[2,2,4,196,768]{4,3,2,1,0:T(8,128)(2,1)}, f32[2,2,4,208,768]{4,3,2,1,0:T(8,128)}, bf16[768,6144]{1,0:T(8,128)(2,1)}, f32[8,768]{1,0:T(8,128)}, f32[8,3072]{1,0:T(8,128)}) custom-call(s32[2]{0:T(128)} %pad_add_fusion.slot_ref.refs_0_, s32[8]{0:T(128)} %reshape.74.live_ref, f32[2,2,4,208,768]{4,3,2,1,0:T(8,128)} %get-tuple-element.56.space_ref, ...), custom_call_target="tpu_custom_call" | custom-call | flops 94220845056 | bytes 62914560 | tf_op jit(solution)/shard_map/mlp/pallas_call | solution.py:728
  403.6 52.2 %spatial_backward.2 = (f32[768,3840]{1,0:T(8,128)}, f32[8,768]{1,0:T(8,128)}, f32[2,4,208,768]{3,2,1,0:T(8,128)}, bf16[2,4,208,768]{3,2,1,0:T(8,128)(2,1)}) custom-call(f32[2,2,4,208,768]{4,3,2,1,0:T(8,128)} %get-tuple-element.58.refs_0_, bf16[2,2,4,208,2304]{4,3,2,1,0:T(8,128)(2,1)} %get-tuple-element.59.refs_1_, ...), custom_call_target="tpu_custom_call" | custom-call | flops 27481079808 | bytes 62914560 | tf_op jit(solution)/shard_map/spatial_backward/pallas_call | solution.py:873
  457.3 53.0 %spatial_backward.3 = (bf16[768,3840]{1,0:T(8,128)(2,1)}, f32[8,768]{1,0:T(8,128)}, f32[2,4,208,768]{3,2,1,0:T(8,128)}, bf16[2,4,208,768]{3,2,1,0:T(8,128)(2,1)}) custom-call(f32[2,2,4,208,768]{4,3,2,1,0:T(8,128)} %get-tuple-element.58.refs_0_, bf16[2,2,4,208,2304]{4,3,2,1,0:T(8,128)(2,1)} %get-tuple-element.59.refs_1_, ...), custom_call_target="tpu_custom_call" | custom-call | flops 27481079808 | bytes 62914560 | tf_op jit(solution)/shard_map/spatial_backward/pallas_call | solution.py:873
  510.3 21.8 %collective-permute-done.2.back_other_ref = bf16[2,4,208,768]{3,2,1,0:T(8,128)(2,1)} collective-permute-done((bf16[2,4,208,768]{3,2,1,0:T(8,128)(2,1)}, bf16[2,4,208,768]{3,2,1,0:T(8,128)(2,1)}, u32[]{:S(2)}, u32[]{:S(2)}) %collective-permute-start.2) | collective-permute-done | bytes 2555936 | tf_op jit(solution)/shard_map/ppermute | solution.py:1133
  532.1 62.6 %temporal_backward.1 = (bf16[768,6272]{1,0:T(8,128)(2,1)}, bf16[2,8,208,2304]{3,2,1,0:T(8,128)(2,1)}) custom-call(s32[2]{0:T(128)} %pad_add_fusion.slot_ref.refs_0_, bf16[2,2,4,196,768]{4,3,2,1,0:T(8,128)(2,1)} %copy.152.own_ref.refs_1_, bf16[2,4,196,768]{3,2,1,0:T(8,128)(2,1)} %copy.148.other_ref.refs_1_, ...), custom_call_target="tpu_custom_call" | custom-call | flops 19629342720 | bytes 62914560 | tf_op jit(solution)/shard_map/temporal_backward/pallas_call | solution.py:1003
  594.8 12.6 %input_grad.2 = bf16[2,4,208,768]{3,2,1,0:T(8,128)(2,1)} custom-call(s32[2]{0:T(128)} %pad_add_fusion.slot_ref.refs_0_, bf16[2,4,196,768]{3,2,1,0:T(8,128)(2,1)} %copy.148.other_ref.refs_1_, bf16[2,8,208,2304]{3,2,1,0:T(8,128)(2,1)} %get-tuple-element.74.refs_2_, f32[16,768]{1,0:T(8,128)} %copy.149.vec_ref.refs_3_.refs_6_, ...), custom_call_target="tpu_custom_call" | custom-call | flops 5888802816 | bytes 20971520 | tf_op jit(solution)/shard_map/input_grad/pallas_call | solution.py:1079
  608.0 6.7 copy.169
  614.7 15.1 %input_grad.3.patch_in_ref = bf16[2,2,4,196,768]{4,3,2,1,0:T(8,128)(2,1)} custom-call(s32[2]{0:T(128)} %pad_add_fusion.slot_ref.refs_0_, bf16[2,2,4,196,768]{4,3,2,1,0:T(8,128)(2,1)} %copy.152.own_ref.refs_1_, bf16[2,8,208,2304]{3,2,1,0:T(8,128)(2,1)} %get-tuple-element.74.refs_2_, f32[16,768]{1,0:T(8,128)} %copy.149.vec_ref.refs_3_.refs_6_, ...), custom_call_target="tpu_custom_call" | custom-call | flops 5888802816 | bytes 20971520 | tf_op jit(solution)/shard_map/input_grad/pallas_call | solution.py:1079
  629.8 45.1 %collective-permute-done.3.back_ref = bf16[2,4,208,768]{3,2,1,0:T(8,128)(2,1)} collective-permute-done((bf16[2,4,208,768]{3,2,1,0:T(8,128)(2,1)}, bf16[2,4,208,768]{3,2,1,0:T(8,128)(2,1)}, u32[]{:S(2)}, u32[]{:S(2)}) %collective-permute-start.3) | collective-permute-done | bytes 2555936 | tf_op jit(solution)/shard_map/ppermute | solution.py:1133
  674.8 5.8 last_sum.1
  680.6 6.5 copy.170
  690.0 44.3 %reduce-scatter.7.cloned.1.call-done = bf16[24,6272]{1,0:T(8,128)(2,1)} async-done(((bf16[768,6272]{1,0:T(8,128)(2,1)}), bf16[24,6272]{1,0:T(8,128)(2,1)}) %reduce-scatter.7.cloned.1.call-update) | async-done | bytes 301072
  (63 shorter events, 31.8 us)
Async XLA Ops:
  7.2 85.2 %all-gather.4.cloned.1.call-start = ((), (), s32[]{:S(2)}) async-start(), calls=%async_computation.2 | async-start | bytes 3852288 | tf_op jit(solution)/shard_map/all_gather | solution.py:1137
  16.4 147.9 %all-gather.6.cloned.1.call-start = ((), (), s32[]{:S(2)}) async-start(), calls=%async_computation.3 | async-start | bytes 6082560 | tf_op jit(solution)/shard_map/all_gather | solution.py:1137
  18.1 240.0 %all-gather.8.cloned.1.call-start = ((), (), s32[]{:S(2)}) async-start(), calls=%async_computation.4 | async-start | bytes 9732096 | tf_op jit(solution)/shard_map/all_gather | solution.py:1137
  21.8 573.0 %reduce-scatter.5.cloned.1.call-start = ((), (), s32[]{:S(2)}) async-start(), calls=%async_computation.5 | async-start | bytes 9732096 | tf_op jit(solution)/shard_map/reduce_scatter | solution.py:1141
  21.8 5.7 copy-start
  24.5 66.2 %collective-permute-start = (bf16[2,4,196,768]{3,1,2,0:T(4,128)(2,1)S(1)}, bf16[2,4,196,768]{3,1,2,0:T(4,128)(2,1)S(1)}, u32[]{:S(2)}, u32[]{:S(2)}) collective-permute-start(bf16[2,4,196,768]{3,1,2,0:T(4,128)(2,1)S(1)} %dynamic-slice_bitcast_fusion), channel_id=1, source_target_pairs={{0,1},{1,0},{2,3},{3,2},{4,5},{5,4},{6,7},{7,6},{8,9},{9,8},{10,11... | collective-permute-start | bytes 7225352 | tf_op jit(solution)/shard_map/ppermute | solution.py:1133
  94.2 46.9 %copy-start.2 = (s32[2]{0:T(128)S(1)}, s32[2]{0:T(128)}, u32[]{:S(2)}) copy-start(s32[2]{0:T(128)} %pad_add_fusion.slot_ref.refs_0_) | copy-start | bytes 28
  94.2 46.9 %copy-start.3 = (s32[2,1]{0,1:T(1,128)S(1)}, s32[2,1]{0,1:T(1,128)}, u32[]{:S(2)}) copy-start(s32[2,1]{0,1:T(1,128)} %param.20) | copy-start | bytes 28
  139.3 74.6 %collective-permute-start.1 = (bf16[2,4,208,768]{3,2,1,0:T(8,128)(2,1)}, bf16[2,4,208,768]{3,2,1,0:T(8,128)(2,1)}, u32[]{:S(2)}, u32[]{:S(2)}) collective-permute-start(bf16[2,4,208,768]{3,2,1,0:T(8,128)(2,1)} %get-tuple-element.49), channel_id=1, source_target_pairs={{0,1},{1,0},{2,3},{3,2},{4,5},{5,4},{6,7},{7,6},{8,9},{9,8},{10,11... | collective-permute-start | bytes 7667720 | tf_op jit(solution)/shard_map/ppermute | solution.py:1133
  403.6 330.7 %reduce-scatter.7.cloned.1.call-start = ((), (), s32[]{:S(2)}) async-start(), calls=%async_computation.6 | async-start | bytes 9934848
  455.8 76.3 %collective-permute-start.2 = (bf16[2,4,208,768]{3,2,1,0:T(8,128)(2,1)}, bf16[2,4,208,768]{3,2,1,0:T(8,128)(2,1)}, u32[]{:S(2)}, u32[]{:S(2)}) collective-permute-start(bf16[2,4,208,768]{3,2,1,0:T(8,128)(2,1)} %get-tuple-element.69), channel_id=1, source_target_pairs={{0,1},{1,0},{2,3},{3,2},{4,5},{5,4},{6,7},{7,6},{8,9},{9,8},{10,11... | collective-permute-start | bytes 7667720 | tf_op jit(solution)/shard_map/ppermute | solution.py:1133
  607.4 67.4 %collective-permute-start.3 = (bf16[2,4,208,768]{3,2,1,0:T(8,128)(2,1)}, bf16[2,4,208,768]{3,2,1,0:T(8,128)(2,1)}, u32[]{:S(2)}, u32[]{:S(2)}) collective-permute-start(bf16[2,4,208,768]{3,2,1,0:T(8,128)(2,1)} %input_grad.2), channel_id=1, source_target_pairs={{0,1},{1,0},{2,3},{3,2},{4,5},{5,4},{6,7},{7,6},{8,9},{9,8},{10,11... | collective-permute-start | bytes 7667720 | tf_op jit(solution)/shard_map/ppermute | solution.py:1133
  680.6 6.5 copy-start.1
Sparse Core Ops, SparseCore 0:
  16.5 72.0 all-gather.3
  92.1 72.1 all-gather.5
  167.8 90.2 all-gather.7
  403.7 147.4 reduce-scatter.4
  594.9 139.3 reduce-scatter.6
